TPU v7x, 32 devices: a whole 2x2x4 slice. The times are simulated.
32 devices in a mesh: outer: 8 (over y, x, core), bisect: 4 (over z).
Axes of the slice: x: 2, y: 2, z: 4, core: 2. Of those that a mesh axis runs over, the one named last changes fastest.
Arguments:
- positions: float32 [3, 32768], P(None, ('outer', 'bisect')), may hold values from -5 to 5, as said below
- masses: float32 [32768], P(('outer', 'bisect')), may hold values from 0.00048828125 to 0.0078125
- velocities: float32 [3, 32768], P(None, ('outer', 'bisect')), may hold values from -4 to 4
- essential: int32 [64, 4], P(('outer', 'bisect')), may hold values from 0 to 7, as said below
- list_count: int32 [64, 4], P('outer', 'bisect'), may hold values from 0 to 4, as said below
- list_target: int32 [64, 4, 4], P('outer', 'bisect'), may hold values from 0 to 7
- list_source: int32 [64, 4, 4], P('outer', 'bisect'), may hold values from 0 to 7
Outputs:
- new_positions: float32 [3, 32768], P(None, ('outer', 'bisect'))
- new_velocities: float32 [3, 32768], P(None, ('outer', 'bisect'))
Inputs may be any that keep to these rules, and one draw needn't show every extreme that they name: `positions`: the volume spans -0.25 to 0.25 along the first component and -5 to 5 along the others. The bodies of device (o, d) lie in its own box of a recursive bisection of the volume: o picks a slab along the first component, and bit b of d halves the box along the second or third component; each block lies in its own sub-box of its device's box. `essential`: the 4 blocks of one device and level are distinct. `list_count`: A domain lists no pairs with its own outer index; some count equals 4 in every draw.
All inputs are finite; a program needn't handle non-finite values.
Results may differ from a plain program's by a relative error of at most 0.0003.
Values sent between devices are 32-bit elements; how exact they have to be, the bound alone decides.
No kernel may reach another device: no remote copies, remote signals or barrier semaphores. Data moves between devices by JAX's collectives and lax.ppermute only.
A program may use at most 64 MiB of HBM per device.

v0:
```python
import jax
import jax.numpy as jnp
from jax import lax
from jax.sharding import PartitionSpec as P

soften_sq = 0.01
time_step = 0.5


def partner(value, axis, bit):
    mask = 2**bit
    pairs = [(source, source ^ mask) for source in range(lax.axis_size(axis))]
    return lax.ppermute(value, axis, pairs)


def pull(targets, sources):
    offset_x = sources[..., 0, None, :] - targets[..., 0, :, None]
    offset_y = sources[..., 1, None, :] - targets[..., 1, :, None]
    offset_z = sources[..., 2, None, :] - targets[..., 2, :, None]
    inverse = lax.rsqrt(offset_x * offset_x + offset_y * offset_y + offset_z * offset_z + soften_sq)
    weight = sources[..., 3, None, :] * inverse * inverse * inverse
    return jnp.stack(
        [
            jnp.sum(weight * offset_x, axis=-1),
            jnp.sum(weight * offset_y, axis=-1),
            jnp.sum(weight * offset_z, axis=-1),
        ],
        axis=-2,
    )


def essential_payload(blocks, chosen):
    picks = (chosen[:, None] == jnp.arange(blocks.shape[0], dtype=jnp.int32)[None, :]).astype(
        jnp.float32
    )
    whole = jnp.einsum("kn,nct->ckt", picks, blocks, precision=lax.Precision.HIGHEST).reshape(4, -1)
    totals = jnp.sum(blocks[:, 3, :], axis=1)
    centre = jnp.sum(blocks[:, :3, :] * blocks[:, 3:4, :], axis=2) / totals[:, None]
    kept = totals * (1.0 - jnp.sum(picks, axis=0))
    monopole = jnp.concatenate([centre.T, kept[None, :]], axis=0)
    return (whole, monopole)


def select_blocks(blocks, wanted):
    picks = (wanted[..., None] == jnp.arange(blocks.shape[0], dtype=wanted.dtype)).astype(
        jnp.float32
    )
    return jnp.einsum("psn,nct->psct", picks, blocks, precision=lax.Precision.HIGHEST)


def pull_items(targets, sources):
    peers, slots = (targets.shape[0], targets.shape[1])
    items = peers * slots
    group = 16
    flat_t = targets.reshape(items // group, group, 3, targets.shape[3])
    flat_s = sources.reshape(items // group, group, 4, sources.shape[3])
    result = lax.map(lambda pair: pull(pair[0], pair[1]), (flat_t, flat_s))
    return result.reshape(peers, slots, 3, targets.shape[3])


def local(positions, masses, velocities, essential, list_count, list_target, list_source):
    bodies = positions.shape[1]
    count_blocks = bodies // 128
    with_mass = jnp.concatenate([positions, masses[None, :]], axis=0)
    blocks = with_mass.reshape(4, count_blocks, 128).transpose(1, 0, 2)
    levels = lax.axis_size("bisect").bit_length() - 1
    wholes = [with_mass]
    monos = []
    for level in range(levels):
        whole, mono = essential_payload(blocks, essential[level])
        got_whole, got_mono = partner((whole, mono), "bisect", level)
        wholes.append(got_whole)
        monos.append(got_mono)
    sources = jnp.concatenate(wholes, axis=1)
    far_points = jnp.concatenate(monos, axis=1)
    tiles = positions.reshape(3, bodies // 256, 256).transpose(1, 0, 2)
    near = lax.map(lambda tile: pull(tile, sources), tiles).transpose(1, 0, 2).reshape(3, bodies)
    far = pull(positions, far_points)
    peers = list_target.shape[0]
    slots = list_target.shape[2]
    target_ids = list_target.reshape(peers, slots)
    source_ids = list_source.reshape(peers, slots)
    picks_t = (target_ids[..., None] == jnp.arange(count_blocks, dtype=jnp.int32)).astype(
        jnp.float32
    )
    targets = jnp.einsum(
        "psn,nct->psct", picks_t, blocks[:, :3, :], precision=lax.Precision.HIGHEST
    )
    valid = (jnp.arange(slots, dtype=jnp.int32)[None, :] < list_count).astype(jnp.float32)
    wanted = lax.all_to_all(source_ids, "outer", split_axis=0, concat_axis=0, tiled=True)
    chosen = select_blocks(blocks, wanted)
    arrived = lax.all_to_all(chosen, "outer", split_axis=0, concat_axis=0, tiled=True)
    remote = pull_items(targets, arrived)
    added = jnp.einsum(
        "psn,psct->nct", picks_t * valid[..., None], remote, precision=lax.Precision.HIGHEST
    )
    added = added.transpose(1, 0, 2).reshape(3, bodies)
    accel = near + far + added
    velocity = velocities + time_step * accel
    position = positions + time_step * velocity
    return (position, velocity)


def solution(mesh):
    placed = (
        P(None, ("outer", "bisect")),
        P(("outer", "bisect")),
        P(None, ("outer", "bisect")),
        P(("outer", "bisect"), None),
        P("outer", "bisect"),
        P("outer", "bisect", None),
        P("outer", "bisect", None),
    )
    return jax.shard_map(
        local,
        mesh=mesh,
        in_specs=placed,
        out_specs=(P(None, ("outer", "bisect")), P(None, ("outer", "bisect"))),
        check_vma=False,
    )
```

profile of v0, /device:TPU:0, one launch (start us, length us, event | category | flops | bytes accessed | tf_op | source)
XLA Modules:
  0.0 34.3 jit_solution(15515202404833851817)
XLA Ops:
  0.7 0.7 %copy.82 = f32[1,3,8,128]{3,2,1,0:T(8,128)S(1)} copy(f32[1,3,8,128]{3,1,2,0:T(4,128)} %bitcast.182) | data formatting | bytes 24576
  1.4 0.7 %fusion.33 = f32[8,4,128]{2,0,1:T(8,128)S(1)} fusion(f32[1,8,128]{2,1,0:T(8,128)} %bitcast.197, f32[3,8,128]{2,1,0:T(8,128)S(1)} %bitcast.192), kind=kLoop, calls=%fused_computation.78 | loop fusion | flops 4096 | bytes 32768 | tf_op jit(solution)/shard_map/transpose | solution.py:65
  2.1 0.1 slice_bitcast_fusion.7
  2.2 0.1 multiply_reduce_fusion
  2.3 0.1 convert_reduce_fusion
  2.4 3.1 %collective-permute-start.2 = (f32[4,8]{1,0:T(4,128)S(1)}, f32[4,8]{1,0:T(4,128)S(1)}, u32[]{:S(2)}, u32[]{:S(2)}) collective-permute-start(f32[4,8]{1,0:T(4,128)S(1)} %get-tuple-element.118), channel_id=1, source_target_pairs={{0,1},{1,0},{2,3},{3,2},{4,5},{5,4},{6,7},{7,6},{8,9},{9,8},{10,11... | collective-permute-start | bytes 392 | tf_op jit(solution)/shard_map/ppermute | solution.py:13
  5.5 2.6 %collective-permute-start.3 = (f32[4,8]{1,0:T(4,128)S(1)}, f32[4,8]{1,0:T(4,128)S(1)}, u32[]{:S(2)}, u32[]{:S(2)}) collective-permute-start(f32[4,8]{1,0:T(4,128)S(1)} %get-tuple-element.119), channel_id=1, source_target_pairs={{0,2},{1,3},{2,0},{3,1},{4,6},{5,7},{6,4},{7,5},{8,10},{9,11},{10,... | collective-permute-start | bytes 392 | tf_op jit(solution)/shard_map/ppermute | solution.py:13
  8.1 0.7 %copy.39 = s32[8,1,4]{2,1,0:T(1,128)} copy(s32[8,1,4]{0,2,1:T(4,128)S(1)} %copy-done.4) | data formatting | bytes 256 | tf_op args[6]
  8.8 3.7 %all-to-all-start = ((s32[8,1,4]{2,1,0:T(1,128)}), s32[8,1,4]{2,1,0:T(1,128)S(1)}, u32[]{:S(2)}, u32[]{:S(2)}) async-start(s32[8,1,4]{2,1,0:T(1,128)} %copy.39), calls=%async_computation | async-start | bytes 8192 | tf_op jit(solution)/shard_map/all_to_all | solution.py:90
  12.5 0.2 convolution_bitcast_fusion.2
  12.7 0.5 %collective-permute-start = (f32[4,512]{1,0:T(4,128)S(1)}, f32[4,512]{1,0:T(4,128)S(1)}, u32[]{:S(2)}, u32[]{:S(2)}) collective-permute-start(f32[4,512]{1,0:T(4,128)S(1)} %bitcast.211), channel_id=1, source_target_pairs={{0,1},{1,0},{2,3},{3,2},{4,5},{5,4},{6,7},{7,6},{8,9},{9,8},{10,11... | collective-permute-start | bytes 24584 | tf_op jit(solution)/shard_map/ppermute | solution.py:13
  13.3 0.2 convolution_bitcast_fusion.1
  13.5 0.4 %collective-permute-start.1 = (f32[4,512]{1,0:T(4,128)S(1)}, f32[4,512]{1,0:T(4,128)S(1)}, u32[]{:S(2)}, u32[]{:S(2)}) collective-permute-start(f32[4,512]{1,0:T(4,128)S(1)} %bitcast.212), channel_id=1, source_target_pairs={{0,2},{1,3},{2,0},{3,1},{4,6},{5,7},{6,4},{7,5},{8,10},{9,11},{10,... | collective-permute-start | bytes 24584 | tf_op jit(solution)/shard_map/ppermute | solution.py:13
  13.9 0.1 copy.50
  14.0 0.2 fusion.34
  14.2 2.9 %all-to-all-done = s32[8,1,4]{2,1,0:T(1,128)S(1)} async-done(((s32[8,1,4]{2,1,0:T(1,128)}), s32[8,1,4]{2,1,0:T(1,128)S(1)}, u32[]{:S(2)}, u32[]{:S(2)}) %all-to-all-start) | async-done | bytes 160 | tf_op jit(solution)/shard_map/all_to_all | solution.py:90
  17.1 0.1 copy.40
  17.2 0.2 fusion.26
  17.4 0.6 %copy.41 = f32[8,4,4,128]{3,2,1,0:T(4,128)} copy(f32[8,4,4,128]{3,0,2,1:T(8,128)S(1)} %fusion.26) | data formatting | bytes 131072 | tf_op jit(solution)/shard_map/psn,nct->psct/dot_general | solution.py:48
  18.1 3.3 %all-to-all-start.1 = ((f32[8,4,4,128]{3,2,1,0:T(4,128)}), f32[8,4,4,128]{3,2,1,0:T(4,128)S(1)}, u32[]{:S(2)}, u32[]{:S(2)}) async-start(f32[8,4,4,128]{3,2,1,0:T(4,128)} %copy.41), calls=%async_computation.1 | async-start | bytes 131072 | tf_op jit(solution)/shard_map/all_to_all | solution.py:92
  21.5 0.1 fusion.20
  21.7 7.1 %while.20 = (s32[]{:T(128)}, f32[4,3,256]{2,1,0:T(4,128)S(1)}, f32[4,2048]{1,0:T(4,128)S(1)}, f32[4,3,256]{2,1,0:T(4,128)S(1)}, s32[]{:T(128)}, /*index=5*/s32[]{:T(128)}, s32[]{}, s32[]{}) while((s32[]{:T(128)}, f32[4,3,256]{2,1,0:T(4,128)S(1)}, f32[4,2048]{1,0:T(4,128)S(1)}, f32[4,3,256]{2,1,0:T(4,128)S(1)}, s32[]{:T(128)}, ...), condition=%wide.region_4.0_spmd, body=%wide.region_0.4_spmd.sunk | while | flops 9437956 | bytes 117885 | solution.py:77
  21.8 1.7 %fusion.62 = (f32[256]{0:T(256)S(1)}, f32[256]{0:T(256)S(1)}, f32[256]{0:T(256)S(1)}) fusion(f32[256]{0:T(256)S(1)} %bitcast.203, f32[2048]{0:T(1024)S(1)} %bitcast.191, f32[256]{0:T(256)S(1)} %bitcast.204, f32[2048]{0:T(1024)S(1)} %bitcast.189, f32[256]{0:T(256)S(1)} %bitcast.202, f32[2048]{0:T(1024)S(1)} %bitcast.190, f32[2048]{0:T(1024)S(1)} %bitcast.188), kind=kLoop, calls=%fused_computation.11.clone.1 | loop fusion | flops 9436416 | bytes 38912 | tf_op jit(solution)/shard_map/while/body/eval_jaxpr/reduce_sum | solution.py:24
  23.6 1.7 %fusion.62 = (f32[256]{0:T(256)S(1)}, f32[256]{0:T(256)S(1)}, f32[256]{0:T(256)S(1)}) fusion(f32[256]{0:T(256)S(1)} %bitcast.203, f32[2048]{0:T(1024)S(1)} %bitcast.191, f32[256]{0:T(256)S(1)} %bitcast.204, f32[2048]{0:T(1024)S(1)} %bitcast.189, f32[256]{0:T(256)S(1)} %bitcast.202, f32[2048]{0:T(1024)S(1)} %bitcast.190, f32[2048]{0:T(1024)S(1)} %bitcast.188), kind=kLoop, calls=%fused_computation.11.clone.1 | loop fusion | flops 9436416 | bytes 38912 | tf_op jit(solution)/shard_map/while/body/eval_jaxpr/reduce_sum | solution.py:24
  25.3 1.7 %fusion.62 = (f32[256]{0:T(256)S(1)}, f32[256]{0:T(256)S(1)}, f32[256]{0:T(256)S(1)}) fusion(f32[256]{0:T(256)S(1)} %bitcast.203, f32[2048]{0:T(1024)S(1)} %bitcast.191, f32[256]{0:T(256)S(1)} %bitcast.204, f32[2048]{0:T(1024)S(1)} %bitcast.189, f32[256]{0:T(256)S(1)} %bitcast.202, f32[2048]{0:T(1024)S(1)} %bitcast.190, f32[2048]{0:T(1024)S(1)} %bitcast.188), kind=kLoop, calls=%fused_computation.11.clone.1 | loop fusion | flops 9436416 | bytes 38912 | tf_op jit(solution)/shard_map/while/body/eval_jaxpr/reduce_sum | solution.py:24
  27.1 1.7 %fusion.62 = (f32[256]{0:T(256)S(1)}, f32[256]{0:T(256)S(1)}, f32[256]{0:T(256)S(1)}) fusion(f32[256]{0:T(256)S(1)} %bitcast.203, f32[2048]{0:T(1024)S(1)} %bitcast.191, f32[256]{0:T(256)S(1)} %bitcast.204, f32[2048]{0:T(1024)S(1)} %bitcast.189, f32[256]{0:T(256)S(1)} %bitcast.202, f32[2048]{0:T(1024)S(1)} %bitcast.190, f32[2048]{0:T(1024)S(1)} %bitcast.188), kind=kLoop, calls=%fused_computation.11.clone.1 | loop fusion | flops 9436416 | bytes 38912 | tf_op jit(solution)/shard_map/while/body/eval_jaxpr/reduce_sum | solution.py:24
  28.8 4.1 %while.21 = (s32[]{:T(128)}, f32[2,16,3,128]{3,1,0,2:T(8,128)S(1)}, f32[2,16,4,128]{3,2,1,0:T(4,128)S(1)}, f32[2,16,3,128]{3,1,0,2:T(8,128)S(1)}, s32[]{:T(128)}) while((s32[]{:T(128)}, f32[2,16,3,128]{3,1,0,2:T(8,128)S(1)}, f32[2,16,4,128]{3,2,1,0:T(4,128)S(1)}, f32[2,16,3,128]{3,1,0,2:T(8,128)S(1)}, s32[]{:T(128)}) %tuple.87), condition=%wide.region_16.17_spmd, body=%wide.region_12.16_spmd.sunk | while | flops 4724738 | bytes 426057 | solution.py:57
  28.9 2.0 %fusion.64 = (f32[16,128]{1,0:T(8,128)S(1)}, f32[16,128]{1,0:T(8,128)S(1)}, f32[16,128]{1,0:T(8,128)S(1)}) fusion(f32[16,128]{1,0:T(8,128)S(1)} %get-tuple-element.206, f32[16,128]{1,0:T(8,128)S(1)} %get-tuple-element.207, f32[16,128]{1,0:T(8,128)S(1)} %get-tuple-element.208, f32[16,128]{1,0:T(8,128)S(1)} %get-tuple-element.209, ...), kind=kLoop, calls=%fused_computation.30.clone.1 | loop fusion | flops 4712448 | bytes 81920 | tf_op jit(solution)/shard_map/while/body/eval_jaxpr/reduce_sum | solution.py:24
  30.9 2.0 %fusion.64 = (f32[16,128]{1,0:T(8,128)S(1)}, f32[16,128]{1,0:T(8,128)S(1)}, f32[16,128]{1,0:T(8,128)S(1)}) fusion(f32[16,128]{1,0:T(8,128)S(1)} %get-tuple-element.206, f32[16,128]{1,0:T(8,128)S(1)} %get-tuple-element.207, f32[16,128]{1,0:T(8,128)S(1)} %get-tuple-element.208, f32[16,128]{1,0:T(8,128)S(1)} %get-tuple-element.209, ...), kind=kLoop, calls=%fused_computation.30.clone.1 | loop fusion | flops 4712448 | bytes 81920 | tf_op jit(solution)/shard_map/while/body/eval_jaxpr/reduce_sum | solution.py:24
  32.9 0.3 convolution_bitcast_fusion
  33.2 0.4 %copy-done.2 = f32[3,1024]{1,0:T(4,128)S(1)} copy-done((f32[3,1024]{1,0:T(4,128)S(1)}, f32[3,1024]{1,0:T(4,128)}, u32[]{:S(2)}) %copy-start.2) | copy-done | bytes 12312
  33.7 0.6 %multiply_add_fusion = (f32[3,1024]{1,0:T(4,128)}, f32[3,1024]{1,0:T(4,128)}) fusion(f32[3,1024]{1,0:T(4,128)S(1)} %bitcast.184, f32[3,1024]{1,0:T(4,128)S(1)} %copy-done.2, f32[1,3,8,128]{3,2,1,0:T(8,128)S(1)} %convolution_bitcast_fusion, f32[3,1024]{1,0:T(4,128)S(1)} %bitcast.208, f32[1,1024]{1,0:T(1,128)S(1)} %bitcast.218, f32[1,1024]{1,0:T(1,128)S(1)} %bitcast.219, ...), kind=kLoop, calls=%fused_computation.72 | loop fusion | flops 24576 | bytes 86016 | tf_op jit(solution)/shard_map/add | solution.py:100
  (54 shorter events, 0.5 us)
Async XLA Ops:
  0.6 1.7 %copy-start.5 = (s32[2,4]{1,0:T(2,128)S(1)}, s32[2,4]{1,0:T(2,128)}, u32[]{:S(2)}) copy-start(s32[2,4]{1,0:T(2,128)} %param.14) | copy-start | bytes 100
  0.6 7.5 %copy-start.4 = (s32[8,1,4]{0,2,1:T(4,128)S(1)}, s32[8,1,4]{0,2,1:T(4,128)}, u32[]{:S(2)}) copy-start(s32[8,1,4]{0,2,1:T(4,128)} %param.17) | copy-start | bytes 388
  0.6 11.9 %copy-start.1 = (f32[1024]{0:T(1024)S(1)}, f32[1024]{0:T(1024)}, u32[]{:S(2)}) copy-start(f32[1024]{0:T(1024)} %param.12) | copy-start | bytes 12292
  2.4 19.0 %collective-permute-start.2 = (f32[4,8]{1,0:T(4,128)S(1)}, f32[4,8]{1,0:T(4,128)S(1)}, u32[]{:S(2)}, u32[]{:S(2)}) collective-permute-start(f32[4,8]{1,0:T(4,128)S(1)} %get-tuple-element.118), channel_id=1, source_target_pairs={{0,1},{1,0},{2,3},{3,2},{4,5},{5,4},{6,7},{7,6},{8,9},{9,8},{10,11... | collective-permute-start | bytes 392 | tf_op jit(solution)/shard_map/ppermute | solution.py:13
  5.5 15.9 %collective-permute-start.3 = (f32[4,8]{1,0:T(4,128)S(1)}, f32[4,8]{1,0:T(4,128)S(1)}, u32[]{:S(2)}, u32[]{:S(2)}) collective-permute-start(f32[4,8]{1,0:T(4,128)S(1)} %get-tuple-element.119), channel_id=1, source_target_pairs={{0,2},{1,3},{2,0},{3,1},{4,6},{5,7},{6,4},{7,5},{8,10},{9,11},{10,... | collective-permute-start | bytes 392 | tf_op jit(solution)/shard_map/ppermute | solution.py:13
  8.8 8.3 %all-to-all-start = ((s32[8,1,4]{2,1,0:T(1,128)}), s32[8,1,4]{2,1,0:T(1,128)S(1)}, u32[]{:S(2)}, u32[]{:S(2)}) async-start(s32[8,1,4]{2,1,0:T(1,128)} %copy.39), calls=%async_computation | async-start | bytes 8192 | tf_op jit(solution)/shard_map/all_to_all | solution.py:90
  12.5 1.3 %copy-start = (f32[3,1024]{1,0:T(4,128)S(1)}, f32[3,1024]{1,0:T(4,128)}, u32[]{:S(2)}) copy-start(f32[3,1024]{1,0:T(4,128)} %param.11) | copy-start | bytes 36868
  12.7 1.2 %copy-start.3 = (s32[8,1,4]{0,2,1:T(4,128)S(1)}, s32[8,1,4]{0,2,1:T(4,128)}, u32[]{:S(2)}) copy-start(s32[8,1,4]{0,2,1:T(4,128)} %param.16) | copy-start | bytes 388
  12.7 8.9 %collective-permute-start = (f32[4,512]{1,0:T(4,128)S(1)}, f32[4,512]{1,0:T(4,128)S(1)}, u32[]{:S(2)}, u32[]{:S(2)}) collective-permute-start(f32[4,512]{1,0:T(4,128)S(1)} %bitcast.211), channel_id=1, source_target_pairs={{0,1},{1,0},{2,3},{3,2},{4,5},{5,4},{6,7},{7,6},{8,9},{9,8},{10,11... | collective-permute-start | bytes 24584 | tf_op jit(solution)/shard_map/ppermute | solution.py:13
  13.5 0.7 %copy-start.6 = (s32[8,1]{0,1:T(1,128)S(1)}, s32[8,1]{0,1:T(1,128)}, u32[]{:S(2)}) copy-start(s32[8,1]{0,1:T(1,128)} %param.15) | copy-start | bytes 100
  13.5 8.2 %collective-permute-start.1 = (f32[4,512]{1,0:T(4,128)S(1)}, f32[4,512]{1,0:T(4,128)S(1)}, u32[]{:S(2)}, u32[]{:S(2)}) collective-permute-start(f32[4,512]{1,0:T(4,128)S(1)} %bitcast.212), channel_id=1, source_target_pairs={{0,2},{1,3},{2,0},{3,1},{4,6},{5,7},{6,4},{7,5},{8,10},{9,11},{10,... | collective-permute-start | bytes 24584 | tf_op jit(solution)/shard_map/ppermute | solution.py:13
  18.1 10.7 %all-to-all-start.1 = ((f32[8,4,4,128]{3,2,1,0:T(4,128)}), f32[8,4,4,128]{3,2,1,0:T(4,128)S(1)}, u32[]{:S(2)}, u32[]{:S(2)}) async-start(f32[8,4,4,128]{3,2,1,0:T(4,128)} %copy.41), calls=%async_computation.1 | async-start | bytes 131072 | tf_op jit(solution)/shard_map/all_to_all | solution.py:92
  32.9 0.7 %copy-start.2 = (f32[3,1024]{1,0:T(4,128)S(1)}, f32[3,1024]{1,0:T(4,128)}, u32[]{:S(2)}) copy-start(f32[3,1024]{1,0:T(4,128)} %param.13) | copy-start | bytes 36868
where the time goes:
time: 34.8 us; the launch traced here: 34.3 us
  starting transfers between devices  13.7 us (39%)
  other arithmetic  12.6 us (36%)
  waiting for transfers between devices  2.95 us (8%)
  local copies, waits for them, and re-layouts  2.93 us (8%)
  matrix products  1.04 us (3%)
  between operations  0.85 us (2%)
    reduce_sum x7, other arithmetic, pull(): jnp.sum(weight * offset_x, axis=-1)  10.8 us
    ppermute x4, starting transfers between devices, partner(): return lax.ppermute(value, axis, pairs)  6.62 us
    all_to_all x1, starting transfers between devices, local(): lax.all_to_all(source_ids, 'outer', split_axis=0, concat_axis=0, tiled=True)  3.72 us
    all_to_all x1, starting transfers between devices, local(): lax.all_to_all(chosen, 'outer', split_axis=0, concat_axis=0, tiled=True)  3.35 us
    all_to_all x1, waiting for transfers between devices, local(): lax.all_to_all(source_ids, 'outer', split_axis=0, concat_axis=0, tiled=True)  2.94 us
    unnamed x18, local copies, waits for them, and re-layouts  1.88 us
  transfers between devices with their start and end apart: 6, of which 1 were waited for; matrix products, arithmetic and copies ran while one was open for 28% of the time, Pallas kernels for 0%

commit v1 on v0

v1 whole, which is shorter than its diff:
```python
import jax
import jax.numpy as jnp
from jax import lax
from jax.experimental import pallas as pl
from jax.experimental.pallas import tpu as pltpu
from jax.sharding import PartitionSpec as P

soften_sq = 0.01
time_step = 0.5
block = 128
f32 = jnp.float32
bf16 = jnp.bfloat16
vmem = pl.BlockSpec(memory_space=pltpu.VMEM)
smem = pl.BlockSpec(memory_space=pltpu.SMEM)


def exchange(value, axis, mask):
    pairs = [(source, source ^ mask) for source in range(lax.axis_size(axis))]
    return lax.ppermute(value, axis, pairs)


def split(value):
    high = value.astype(bf16).astype(f32)
    rest = value - high
    mid = rest.astype(bf16).astype(f32)
    return high, mid, rest - mid


def target_rows(points):
    high, mid, low = split(-2.0 * points[0:3])
    norm = jnp.sum(points[0:3] * points[0:3], axis=0, keepdims=True) + soften_sq
    one = jnp.ones_like(norm)
    return jnp.concatenate([high, mid, low, high, mid, high, one, one, one, *split(norm)], 0).astype(bf16)


def source_rows(points):
    high, mid, low = split(points[0:3])
    norm = jnp.sum(points[0:3] * points[0:3], axis=0, keepdims=True)
    one = jnp.ones_like(norm)
    return jnp.concatenate([high, high, high, mid, mid, low, *split(norm), one, one, one], 0).astype(bf16)


def moment_rows(points):
    moments = jnp.concatenate([points[0:3] * points[3:4], points[3:4]], 0)
    return jnp.concatenate([*split(moments), jnp.zeros_like(moments)], 0).astype(bf16)


def pull(columns, moments, targets):
    dist = jnp.dot(columns, targets, preferred_element_type=f32)
    inverse = lax.rsqrt(dist)
    weight = inverse * inverse * inverse
    high = weight.astype(bf16)
    low = (weight - high.astype(f32)).astype(bf16)
    return jnp.dot(moments, high, preferred_element_type=f32) + jnp.dot(
        moments, low, preferred_element_type=f32
    )


def flip(rows):
    return jnp.transpose(rows.astype(f32)).astype(bf16)


def pull_all(columns, moments, targets, step=256):
    parts = []
    for start in range(0, targets.shape[1], step):
        acc = None
        for first in range(0, columns.shape[0], step):
            part = pull(
                columns[first : first + step],
                moments[:, first : first + step],
                targets[:, start : start + step],
            )
            acc = part if acc is None else acc + part
        parts.append(acc)
    return jnp.concatenate(parts, 1)


def own_kernel(own_ref, out_ref):
    own = own_ref[:, : out_ref.shape[1]]
    out_ref[...] = pull_all(flip(source_rows(own)), moment_rows(own), target_rows(own))


def partner_kernel(picks, own_ref, other_ref, level, sums_ref, out_ref):
    bodies = out_ref.shape[1]
    count = bodies // block
    other = other_ref[:, :bodies]
    lane = lax.broadcasted_iota(jnp.int32, (1, block), 1)
    ids = other_ref[level : level + 1, bodies : bodies + block]
    power = jnp.zeros((1, block), f32)
    for pick in range(picks):
        power = jnp.where(lane == pick, float(count**pick), power)
    code = jnp.sum(ids * power).astype(jnp.int32)
    chosen = [(code // count**pick) % count for pick in range(picks)]
    moments = moment_rows(other)
    body = lax.broadcasted_iota(jnp.int32, (bodies, block), 0) // block
    place = lax.broadcasted_iota(jnp.int32, (bodies, block), 1)
    member = (body == place).astype(f32).astype(bf16)
    totals = jnp.dot(moments, member, preferred_element_type=f32)
    totals = totals[0:4] + totals[4:8] + totals[8:12]
    kept = lane < count
    for pick in chosen:
        kept = kept & (lane != pick)
    mass = jnp.where(lane < count, totals[3:4], 1.0)
    mono = jnp.concatenate([totals[0:3] / mass, jnp.where(kept, totals[3:4], 0.0)], 0)
    near = [other_ref[:, pl.ds(pl.multiple_of(pick * block, block), block)] for pick in chosen]
    points = jnp.concatenate(near + [mono], 1)
    whole = picks * block
    columns = flip(source_rows(points))
    moments = moment_rows(points)
    targets = target_rows(own_ref[:, :bodies])
    near = pull_all(columns[:whole], moments[:, :whole], targets)
    far = pull(columns[whole : whole + 16], moments[:, whole : whole + 16], targets)
    out_ref[...] = sums_ref[...] + near + far


def remote_kernel(here_ref, there_ref, count_ref, target_ref, source_ref, sums_ref, speed_ref,
                  position_ref, velocity_ref, rows_ref, acc_ref):
    bodies = sums_ref.shape[1]
    slots = target_ref.shape[1]
    place = lax.axis_index("outer")
    own = here_ref[0, :, :bodies]
    rows_ref[...] = target_rows(own)
    acc_ref[...] = sums_ref[...]
    half = here_ref.shape[0]

    def peer(group_ref, index, mask):
        other = place ^ mask
        points = []
        for slot in range(slots):
            start = pl.multiple_of(source_ref[other, slot] * block, block)
            points.append(group_ref[index, :, pl.ds(start, block)])
        points = jnp.concatenate(points, 1)
        columns = flip(source_rows(points))
        moments = moment_rows(points)
        for slot in range(slots):
            start = pl.multiple_of(target_ref[other, slot] * block, block)
            span = slice(slot * block, (slot + 1) * block)
            part = pull(columns[span], moments[:, span], rows_ref[:, pl.ds(start, block)])
            valid = jnp.where(slot < count_ref[other, 0], 1.0, 0.0)
            acc_ref[:, pl.ds(start, block)] += part * valid

    for index in range(1, half):
        peer(here_ref, index, 2 * index)
    for index in range(half):
        peer(there_ref, index, 2 * index + 1)
    total = acc_ref[0:4] + acc_ref[4:8] + acc_ref[8:12]
    position = own[0:3]
    velocity = speed_ref[...] + time_step * (total[0:3] - position * total[3:4])
    velocity_ref[...] = velocity
    position_ref[...] = position + time_step * velocity


def local(positions, masses, velocities, essential, list_count, list_target, list_source):
    bodies = positions.shape[1]
    levels = lax.axis_size("bisect").bit_length() - 1
    peers = lax.axis_size("outer")
    picks = essential.shape[1]
    slots = list_target.shape[2]
    sums = jax.ShapeDtypeStruct((16, bodies), f32)
    ids = jnp.pad(essential.astype(f32), ((0, 4 - levels), (0, block - picks)))
    own = jnp.concatenate([jnp.concatenate([positions, masses[None, :]], 0), ids], 1)
    across = [exchange(own, "bisect", 1 << level) for level in range(levels)]
    here = [own] + [exchange(own, "outer", mask) for mask in range(2, peers, 2)]
    here = jnp.stack(here)
    there = exchange(here, "outer", 1)
    acc = pl.pallas_call(own_kernel, out_shape=sums, in_specs=[vmem], out_specs=vmem)(own)
    for level in range(levels):
        acc = pl.pallas_call(
            lambda own_ref, other_ref, sums_ref, out_ref, level=level: partner_kernel(
                picks, own_ref, other_ref, level, sums_ref, out_ref
            ),
            out_shape=sums,
            in_specs=[vmem] * 3,
            out_specs=vmem,
        )(own, across[level], acc)
    shape = jax.ShapeDtypeStruct((3, bodies), f32)
    return pl.pallas_call(
        remote_kernel,
        out_shape=(shape, shape),
        in_specs=[vmem, vmem, smem, smem, smem, vmem, vmem],
        out_specs=(vmem, vmem),
        scratch_shapes=[pltpu.VMEM((24, bodies), bf16), pltpu.VMEM((16, bodies), f32)],
    )(here, there, list_count, list_target.reshape(peers, slots), list_source.reshape(peers, slots),
      acc, velocities)


def solution(mesh):
    placed = (
        P(None, ("outer", "bisect")),
        P(("outer", "bisect")),
        P(None, ("outer", "bisect")),
        P(("outer", "bisect"), None),
        P("outer", "bisect"),
        P("outer", "bisect", None),
        P("outer", "bisect", None),
    )
    return jax.shard_map(
        local,
        mesh=mesh,
        in_specs=placed,
        out_specs=(P(None, ("outer", "bisect")), P(None, ("outer", "bisect"))),
        check_vma=False,
    )
```

time: 34.8 us -> 32.8 us (0.943)
  Pallas kernels: 0 us -> 12.8 us
  other arithmetic: 12.6 us -> 1.45 us
  starting transfers between devices: 13.7 us -> 8.87 us
  waiting for transfers between devices: 2.95 us -> 4.65 us
  matrix products: 1.04 us -> 0 us
  local copies, waits for them, and re-layouts: 2.93 us -> 3.85 us
    pallas_call x0 -> x4, Pallas kernels: none -> 12.8 us  [the longest x2 5.67 us: local(): pl.pallas_call(lambda own_ref, other_ref, sums_ref, out_ref, level=level:...]
    reduce_sum x9 -> x0, other arithmetic: 10.9 us -> none  [the longest x7 10.8 us: pull(): jnp.sum(weight * offset_x, axis=-1)]
    all_to_all x2 -> x0, starting transfers between devices: 7.07 us -> none  [the longest x1 3.72 us: local(): lax.all_to_all(source_ids, 'outer', split_axis=0, concat_axis=0, tiled=True)]
    ppermute x4 -> x6, waiting for transfers between devices: 0.01 us -> 4.65 us  [exchange(): return lax.ppermute(value, axis, pairs)]
    all_to_all x2 -> x0, waiting for transfers between devices: 2.94 us -> none  [the longest x1 2.94 us: local(): lax.all_to_all(source_ids, 'outer', split_axis=0, concat_axis=0, tiled=True)]
    ppermute x4 -> x6, starting transfers between devices: 6.62 us -> 8.87 us  [exchange(): return lax.ppermute(value, axis, pairs)]
    reshape x0 -> x2, local copies, waits for them, and re-layouts: none -> 1.34 us  [the longest x1 0.67 us: local(): list_target.reshape(peers, slots)]
    dot_general x5 -> x0, matrix products: 1.04 us -> none  [the longest x2 0.38 us: essential_payload(): jnp.einsum('kn,nct->ckt', picks, blocks, precision=lax.Precision.HIGHEST)]
  transfers between devices with their start and end apart: 6 -> 6, of which waited for: 1 -> 3; matrix products, arithmetic and copies ran while one was open for 28% -> 6% of each run, Pallas kernels for 0% -> 26%
where the time goes in v1:
time: 32.8 us; the launch traced here: 32.3 us
  Pallas kernels  12.8 us (39%)
  starting transfers between devices  8.87 us (27%)
  waiting for transfers between devices  4.65 us (14%)
  local copies, waits for them, and re-layouts  3.85 us (12%)
  other arithmetic  1.45 us (4%)
  between operations  0.68 us (2%)
    ppermute x6, starting transfers between devices, exchange(): return lax.ppermute(value, axis, pairs)  8.87 us
    pallas_call x2, Pallas kernels, local(): pl.pallas_call(lambda own_ref, other_ref, sums_ref, out_ref, level=level:...  5.67 us
    ppermute x6, waiting for transfers between devices, exchange(): return lax.ppermute(value, axis, pairs)  4.65 us
    pallas_call x1, Pallas kernels, local(): pl.pallas_call(remote_kernel, out_shape=(shape, shape), in_specs=[vmem, v...  4.35 us
    pallas_call x1, Pallas kernels, local(): pl.pallas_call(own_kernel, out_shape=sums, in_specs=[vmem], out_specs=vmem)  2.81 us
    unnamed x17, local copies, waits for them, and re-layouts  2.51 us
    concatenate x1, other arithmetic, local(): jnp.concatenate([jnp.concatenate([positions, masses[None, :]], 0), ids], 1)  0.74 us
    convert_element_type x1, other arithmetic, local(): ids = jnp.pad(essential.astype(f32), ((0, 4 - levels), (0, block - picks)))  0.68 us
  transfers between devices with their start and end apart: 6, of which 3 were waited for; matrix products, arithmetic and copies ran while one was open for 6% of the time, Pallas kernels for 26%

profile of v1, /device:TPU:0, one launch (start us, length us, event | category | flops | bytes accessed | tf_op | source)
XLA Modules:
  0.0 32.3 jit_solution(4332754817933837035)
XLA Ops:
  0.6 0.7 %convert_element_type.5 = f32[2,4]{1,0:T(2,128)S(1)} convert(s32[2,4]{1,0:T(2,128)} %param.10) | non-fusion elementwise | flops 8 | bytes 64 | tf_op jit(solution)/shard_map/convert_element_type | solution.py:160
  1.3 0.7 %select_maximum_fusion.own_ref = f32[4,1152]{1,0:T(4,128)S(1)} fusion(f32[2,4]{1,0:T(2,128)S(1)} %convert_element_type.5, f32[1,1024]{1,0:T(1,128)} %bitcast.11, f32[3,1024]{1,0:T(4,128)} %param.7), kind=kLoop, calls=%fused_computation.1 | loop fusion | flops 18432 | bytes 34848 | tf_op jit(solution)/shard_map/concatenate | solution.py:161
  2.1 0.0 copy-start
  2.1 3.0 %collective-permute-start = (f32[4,1152]{1,0:T(4,128)S(1)}, f32[4,1152]{1,0:T(4,128)S(1)}, u32[]{:S(2)}, u32[]{:S(2)}) collective-permute-start(f32[4,1152]{1,0:T(4,128)S(1)} %select_maximum_fusion.own_ref), channel_id=1, source_target_pairs={{0,8},{4,12},{8,0},{12,4},{16,24},{20,28},{24,16},{28,20},{1,9},{5... | collective-permute-start | bytes 55304 | tf_op jit(solution)/shard_map/ppermute | solution.py:19
  5.1 1.5 %collective-permute-start.1 = (f32[4,1152]{1,0:T(4,128)S(1)}, f32[4,1152]{1,0:T(4,128)S(1)}, u32[]{:S(2)}, u32[]{:S(2)}) collective-permute-start(f32[4,1152]{1,0:T(4,128)S(1)} %select_maximum_fusion.own_ref), channel_id=1, source_target_pairs={{0,16},{4,20},{8,24},{12,28},{16,0},{20,4},{24,8},{28,12},{1,17},{... | collective-permute-start | bytes 55304 | tf_op jit(solution)/shard_map/ppermute | solution.py:19
  6.6 0.0 collective-permute-start.2
  6.6 0.2 collective-permute-done
  6.8 2.0 %collective-permute-done.1 = f32[4,1152]{1,0:T(4,128)S(1)} collective-permute-done((f32[4,1152]{1,0:T(4,128)S(1)}, f32[4,1152]{1,0:T(4,128)S(1)}, u32[]{:S(2)}, u32[]{:S(2)}) %collective-permute-start.1) | collective-permute-done | bytes 18464 | tf_op jit(solution)/shard_map/ppermute | solution.py:19
  8.9 2.4 %collective-permute-done.2 = f32[4,1152]{1,0:T(4,128)S(1)} collective-permute-done((f32[4,1152]{1,0:T(4,128)S(1)}, f32[4,1152]{1,0:T(4,128)S(1)}, u32[]{:S(2)}, u32[]{:S(2)}) %collective-permute-start.2) | collective-permute-done | bytes 18464 | tf_op jit(solution)/shard_map/ppermute | solution.py:19
  11.3 0.0 copy-start.1
  11.3 0.1 collective-permute-start.3
  11.4 1.6 %collective-permute-start.5 = (f32[4,1152]{1,0:T(4,128)S(1)}, f32[4,1152]{1,0:T(4,128)S(1)}, u32[]{:S(2)}, u32[]{:S(2)}) collective-permute-start(f32[4,1152]{1,0:T(4,128)S(1)} %select_maximum_fusion.own_ref), channel_id=1, source_target_pairs={{0,1},{1,0},{2,3},{3,2},{4,5},{5,4},{6,7},{7,6},{8,9},{9,8},{10,11... | collective-permute-start | bytes 55304 | tf_op jit(solution)/shard_map/ppermute | solution.py:19
  13.0 0.0 copy-done
  13.0 2.6 %collective-permute-start.4 = (f32[4,1152]{1,0:T(4,128)S(1)}, f32[4,1152]{1,0:T(4,128)S(1)}, u32[]{:S(2)}, u32[]{:S(2)}) collective-permute-start(f32[4,1152]{1,0:T(4,128)S(1)} %select_maximum_fusion.own_ref), channel_id=1, source_target_pairs={{0,2},{1,3},{2,0},{3,1},{4,6},{5,7},{6,4},{7,5},{8,10},{9,11},{10,... | collective-permute-start | bytes 55304 | tf_op jit(solution)/shard_map/ppermute | solution.py:19
  15.6 0.0 copy-start.5
  15.6 2.8 %shard_map.86.sums_ref = f32[16,1024]{1,0:T(8,128)} custom-call(f32[4,1152]{1,0:T(4,128)} %copy-done), custom_call_target="tpu_custom_call" | custom-call | tf_op jit(solution)/shard_map/pallas_call | solution.py:166
  18.4 0.0 copy-done.5
  18.4 0.7 %copy.10.target_ref = s32[8,4]{1,0:T(8,128)} copy(s32[8,4]{0,1:T(4,128)S(1)} %bitcast.12) | data formatting | bytes 256 | tf_op jit(solution)/shard_map/reshape | solution.py:183
  19.1 0.0 copy-done.6
  19.1 0.7 %copy.11.source_ref = s32[8,4]{1,0:T(8,128)} copy(s32[8,4]{0,1:T(4,128)S(1)} %bitcast.13) | data formatting | bytes 256 | tf_op jit(solution)/shard_map/reshape | solution.py:183
  19.8 0.0 copy-done.7
  19.8 0.7 %copy.9.count_ref = s32[8,1]{1,0:T(8,128)} copy(s32[8,1]{0,1:T(1,128)S(1)} %copy-done.7) | data formatting | bytes 64 | tf_op args[4]
  20.5 0.0 collective-permute-done.5.other_ref
  20.5 0.6 %copy-done.4 = f32[4,1152]{1,0:T(4,128)} copy-done((f32[4,1152]{1,0:T(4,128)}, f32[4,1152]{1,0:T(4,128)S(1)}, u32[]{:S(2)}) %copy-start.4) | copy-done | bytes 18456
  21.1 2.8 %shard_map.87.sums_ref = f32[16,1024]{1,0:T(8,128)} custom-call(f32[4,1152]{1,0:T(4,128)} %copy-done, f32[4,1152]{1,0:T(4,128)} %copy-done.4, f32[16,1024]{1,0:T(8,128)} %shard_map.86.sums_ref), custom_call_target="tpu_custom_call" | custom-call | tf_op jit(solution)/shard_map/pallas_call | solution.py:168
  23.9 0.0 copy-done.1
  23.9 0.0 collective-permute-done.4.other_ref
  23.9 0.6 %copy-done.3 = f32[4,1152]{1,0:T(4,128)} copy-done((f32[4,1152]{1,0:T(4,128)}, f32[4,1152]{1,0:T(4,128)S(1)}, u32[]{:S(2)}) %copy-start.3) | copy-done | bytes 18456
  24.5 2.8 %shard_map.88.sums_ref = f32[16,1024]{1,0:T(8,128)} custom-call(f32[4,1152]{1,0:T(4,128)} %copy-done, f32[4,1152]{1,0:T(4,128)} %copy-done.3, f32[16,1024]{1,0:T(8,128)} %shard_map.87.sums_ref), custom_call_target="tpu_custom_call" | custom-call | tf_op jit(solution)/shard_map/pallas_call | solution.py:168
  27.4 0.0 collective-permute-done.3.there_ref
  27.4 0.6 %copy-done.2 = f32[4,4,1152]{2,1,0:T(4,128)} copy-done((f32[4,4,1152]{2,1,0:T(4,128)}, f32[4,4,1152]{2,1,0:T(4,128)S(1)}, u32[]{:S(2)}) %copy-start.2) | copy-done | bytes 73752
  28.0 4.4 %shard_map.89 = (f32[3,1024]{1,0:T(4,128)}, f32[3,1024]{1,0:T(4,128)}) custom-call(f32[4,4,1152]{2,1,0:T(4,128)} %copy-done.1, f32[4,4,1152]{2,1,0:T(4,128)} %copy-done.2, s32[8,1]{1,0:T(8,128)} %copy.9.count_ref, s32[8,4]{1,0:T(8,128)} %copy.10.target_ref, s32[8,4]{1,0:T(8,128)} %copy.11.source_ref, f32[16,1024]{1,0:T(8,128)} %shard_map.88.sums_ref, ...), custom_call_target="tpu_custom_call" | custom-call | tf_op jit(solution)/shard_map/pallas_call | solution.py:177
  (6 shorter events, 0.0 us)
Async XLA Ops:
  2.1 11.0 %copy-start = (f32[4,1152]{1,0:T(4,128)}, f32[4,1152]{1,0:T(4,128)S(1)}, u32[]{:S(2)}) copy-start(f32[4,1152]{1,0:T(4,128)S(1)} %select_maximum_fusion.own_ref) | copy-start | bytes 55300
  2.1 4.8 %collective-permute-start = (f32[4,1152]{1,0:T(4,128)S(1)}, f32[4,1152]{1,0:T(4,128)S(1)}, u32[]{:S(2)}, u32[]{:S(2)}) collective-permute-start(f32[4,1152]{1,0:T(4,128)S(1)} %select_maximum_fusion.own_ref), channel_id=1, source_target_pairs={{0,8},{4,12},{8,0},{12,4},{16,24},{20,28},{24,16},{28,20},{1,9},{5... | collective-permute-start | bytes 55304 | tf_op jit(solution)/shard_map/ppermute | solution.py:19
  5.1 3.8 %collective-permute-start.1 = (f32[4,1152]{1,0:T(4,128)S(1)}, f32[4,1152]{1,0:T(4,128)S(1)}, u32[]{:S(2)}, u32[]{:S(2)}) collective-permute-start(f32[4,1152]{1,0:T(4,128)S(1)} %select_maximum_fusion.own_ref), channel_id=1, source_target_pairs={{0,16},{4,20},{8,24},{12,28},{16,0},{20,4},{24,8},{28,12},{1,17},{... | collective-permute-start | bytes 55304 | tf_op jit(solution)/shard_map/ppermute | solution.py:19
  6.6 4.7 %collective-permute-start.2 = (f32[4,1152]{1,0:T(4,128)S(1)}, f32[4,1152]{1,0:T(4,128)S(1)}, u32[]{:S(2)}, u32[]{:S(2)}) collective-permute-start(f32[4,1152]{1,0:T(4,128)S(1)} %select_maximum_fusion.own_ref), channel_id=1, source_target_pairs={{0,24},{4,28},{8,16},{12,20},{16,8},{20,12},{24,0},{28,4},{1,25},{... | collective-permute-start | bytes 55304 | tf_op jit(solution)/shard_map/ppermute | solution.py:19
  11.3 12.6 %copy-start.1 = (f32[4,4,1152]{2,1,0:T(4,128)}, f32[4,4,1152]{2,1,0:T(4,128)S(1)}, u32[]{:S(2)}) copy-start(f32[4,4,1152]{2,1,0:T(4,128)S(1)} %pad_maximum_fusion.here_ref) | copy-start | bytes 221188
  11.3 16.0 %collective-permute-start.3 = (f32[4,4,1152]{2,1,0:T(4,128)S(1)}, f32[4,4,1152]{2,1,0:T(4,128)S(1)}, u32[]{:S(2)}, u32[]{:S(2)}) collective-permute-start(f32[4,4,1152]{2,1,0:T(4,128)S(1)} %pad_maximum_fusion.here_ref), channel_id=1, source_target_pairs={{0,4},{4,0},{8,12},{12,8},{16,20},{20,16},{24,28},{28,24},{1,5},{5... | collective-permute-start | bytes 221192 | tf_op jit(solution)/shard_map/ppermute | solution.py:19
  11.4 9.1 %collective-permute-start.5 = (f32[4,1152]{1,0:T(4,128)S(1)}, f32[4,1152]{1,0:T(4,128)S(1)}, u32[]{:S(2)}, u32[]{:S(2)}) collective-permute-start(f32[4,1152]{1,0:T(4,128)S(1)} %select_maximum_fusion.own_ref), channel_id=1, source_target_pairs={{0,1},{1,0},{2,3},{3,2},{4,5},{5,4},{6,7},{7,6},{8,9},{9,8},{10,11... | collective-permute-start | bytes 55304 | tf_op jit(solution)/shard_map/ppermute | solution.py:19
  13.0 10.9 %collective-permute-start.4 = (f32[4,1152]{1,0:T(4,128)S(1)}, f32[4,1152]{1,0:T(4,128)S(1)}, u32[]{:S(2)}, u32[]{:S(2)}) collective-permute-start(f32[4,1152]{1,0:T(4,128)S(1)} %select_maximum_fusion.own_ref), channel_id=1, source_target_pairs={{0,2},{1,3},{2,0},{3,1},{4,6},{5,7},{6,4},{7,5},{8,10},{9,11},{10,... | collective-permute-start | bytes 55304 | tf_op jit(solution)/shard_map/ppermute | solution.py:19
  15.6 2.8 %copy-start.5 = (s32[8,1,4]{0,2,1:T(4,128)S(1)}, s32[8,1,4]{0,2,1:T(4,128)}, u32[]{:S(2)}) copy-start(s32[8,1,4]{0,2,1:T(4,128)} %param.12) | copy-start | bytes 388
  18.4 0.7 %copy-start.6 = (s32[8,1,4]{0,2,1:T(4,128)S(1)}, s32[8,1,4]{0,2,1:T(4,128)}, u32[]{:S(2)}) copy-start(s32[8,1,4]{0,2,1:T(4,128)} %param.13) | copy-start | bytes 388
  19.1 0.7 %copy-start.7 = (s32[8,1]{0,1:T(1,128)S(1)}, s32[8,1]{0,1:T(1,128)}, u32[]{:S(2)}) copy-start(s32[8,1]{0,1:T(1,128)} %param.11) | copy-start | bytes 100
  20.5 0.6 %copy-start.4 = (f32[4,1152]{1,0:T(4,128)}, f32[4,1152]{1,0:T(4,128)S(1)}, u32[]{:S(2)}) copy-start(f32[4,1152]{1,0:T(4,128)S(1)} %collective-permute-done.5.other_ref) | copy-start | bytes 55300
  23.9 0.6 %copy-start.3 = (f32[4,1152]{1,0:T(4,128)}, f32[4,1152]{1,0:T(4,128)S(1)}, u32[]{:S(2)}) copy-start(f32[4,1152]{1,0:T(4,128)S(1)} %collective-permute-done.4.other_ref) | copy-start | bytes 55300
  27.4 0.6 %copy-start.2 = (f32[4,4,1152]{2,1,0:T(4,128)}, f32[4,4,1152]{2,1,0:T(4,128)S(1)}, u32[]{:S(2)}) copy-start(f32[4,4,1152]{2,1,0:T(4,128)S(1)} %collective-permute-done.3.there_ref) | copy-start | bytes 221188

commit v2 on v1

--- a/solution.py
+++ b/solution.py
@@ -4,6 +4,7 @@
 from jax.experimental import pallas as pl
 from jax.experimental.pallas import tpu as pltpu
 from jax.sharding import PartitionSpec as P
+
 
 soften_sq = 0.01
 time_step = 0.5
@@ -75,6 +76,26 @@
     return jnp.concatenate(parts, 1)
 
 
+def kept(value):
+    return pltpu.with_memory_space_constraint(value, pltpu.VMEM)
+
+
+def pack_kernel(essential_ref, position_ref, mass_ref, own_ref):
+    levels, picks = essential_ref.shape
+    bodies = position_ref.shape[1]
+    count = bodies // block
+    own_ref[0:3, :bodies] = position_ref[...]
+    own_ref[3:4, :bodies] = mass_ref[...]
+    row = lax.broadcasted_iota(jnp.int32, (4, block), 0)
+    codes = jnp.zeros((4, block), f32)
+    for level in range(levels):
+        code = 0
+        for pick in range(picks):
+            code = code * count + essential_ref[level, pick]
+        codes = jnp.where(row == level, code.astype(f32), codes)
+    own_ref[:, bodies:] = codes
+
+
 def own_kernel(own_ref, out_ref):
     own = own_ref[:, : out_ref.shape[1]]
     out_ref[...] = pull_all(flip(source_rows(own)), moment_rows(own), target_rows(own))
@@ -85,11 +106,7 @@
     count = bodies // block
     other = other_ref[:, :bodies]
     lane = lax.broadcasted_iota(jnp.int32, (1, block), 1)
-    ids = other_ref[level : level + 1, bodies : bodies + block]
-    power = jnp.zeros((1, block), f32)
-    for pick in range(picks):
-        power = jnp.where(lane == pick, float(count**pick), power)
-    code = jnp.sum(ids * power).astype(jnp.int32)
+    code = jnp.max(other_ref[level : level + 1, bodies : bodies + block]).astype(jnp.int32)
     chosen = [(code // count**pick) % count for pick in range(picks)]
     moments = moment_rows(other)
     body = lax.broadcasted_iota(jnp.int32, (bodies, block), 0) // block
@@ -116,7 +133,7 @@
 def remote_kernel(here_ref, there_ref, count_ref, target_ref, source_ref, sums_ref, speed_ref,
                   position_ref, velocity_ref, rows_ref, acc_ref):
     bodies = sums_ref.shape[1]
-    slots = target_ref.shape[1]
+    slots = target_ref.shape[0]
     place = lax.axis_index("outer")
     own = here_ref[0, :, :bodies]
     rows_ref[...] = target_rows(own)
@@ -127,16 +144,16 @@
         other = place ^ mask
         points = []
         for slot in range(slots):
-            start = pl.multiple_of(source_ref[other, slot] * block, block)
+            start = pl.multiple_of(source_ref[slot, other] * block, block)
             points.append(group_ref[index, :, pl.ds(start, block)])
         points = jnp.concatenate(points, 1)
         columns = flip(source_rows(points))
         moments = moment_rows(points)
         for slot in range(slots):
-            start = pl.multiple_of(target_ref[other, slot] * block, block)
+            start = pl.multiple_of(target_ref[slot, other] * block, block)
             span = slice(slot * block, (slot + 1) * block)
             part = pull(columns[span], moments[:, span], rows_ref[:, pl.ds(start, block)])
-            valid = jnp.where(slot < count_ref[other, 0], 1.0, 0.0)
+            valid = jnp.where(slot < count_ref[0, other], 1.0, 0.0)
             acc_ref[:, pl.ds(start, block)] += part * valid
 
     for index in range(1, half):
@@ -156,14 +173,22 @@
     peers = lax.axis_size("outer")
     picks = essential.shape[1]
     slots = list_target.shape[2]
-    sums = jax.ShapeDtypeStruct((16, bodies), f32)
-    ids = jnp.pad(essential.astype(f32), ((0, 4 - levels), (0, block - picks)))
-    own = jnp.concatenate([jnp.concatenate([positions, masses[None, :]], 0), ids], 1)
-    across = [exchange(own, "bisect", 1 << level) for level in range(levels)]
-    here = [own] + [exchange(own, "outer", mask) for mask in range(2, peers, 2)]
+    sums = pltpu.VMEM((16, bodies), f32)
+    own = pl.pallas_call(
+        pack_kernel,
+        out_shape=pltpu.VMEM((4, bodies + block), f32),
+        in_specs=[smem, vmem, vmem],
+        out_specs=vmem,
+    )(essential, positions, masses.reshape(1, bodies))
+    across = []
+    for level in range(levels):
+        across.append(exchange(own, "bisect", 1 << level))
+    here = [own]
+    for mask in range(2, peers, 2):
+        here.append(exchange(own, "outer", mask))
     here = jnp.stack(here)
     there = exchange(here, "outer", 1)
-    acc = pl.pallas_call(own_kernel, out_shape=sums, in_specs=[vmem], out_specs=vmem)(own)
+    acc = pl.pallas_call(own_kernel, out_shape=sums, in_specs=[vmem], out_specs=vmem)(kept(own))
     for level in range(levels):
         acc = pl.pallas_call(
             lambda own_ref, other_ref, sums_ref, out_ref, level=level: partner_kernel(
@@ -172,7 +197,7 @@
             out_shape=sums,
             in_specs=[vmem] * 3,
             out_specs=vmem,
-        )(own, across[level], acc)
+        )(kept(own), kept(across[level]), kept(acc))
     shape = jax.ShapeDtypeStruct((3, bodies), f32)
     return pl.pallas_call(
         remote_kernel,
@@ -180,8 +205,15 @@
         in_specs=[vmem, vmem, smem, smem, smem, vmem, vmem],
         out_specs=(vmem, vmem),
         scratch_shapes=[pltpu.VMEM((24, bodies), bf16), pltpu.VMEM((16, bodies), f32)],
-    )(here, there, list_count, list_target.reshape(peers, slots), list_source.reshape(peers, slots),
-      acc, velocities)
+    )(
+        kept(here),
+        kept(there),
+        list_count.T,
+        list_target.reshape(peers, slots).T,
+        list_source.reshape(peers, slots).T,
+        kept(acc),
+        velocities,
+    )
 
 
 def solution(mesh):

time: 32.8 us -> 23.4 us (0.71)
  local copies, waits for them, and re-layouts: 3.85 us -> 0 us
  Pallas kernels: 12.8 us -> 8.97 us
  other arithmetic: 1.45 us -> 0.02 us
    pallas_call x2, Pallas kernels: 5.67 us -> 2.68 us  [local(): pl.pallas_call(lambda own_ref, other_ref, sums_ref, out_ref, level=level:...]
    unnamed x17 -> x0, local copies, waits for them, and re-layouts: 2.51 us -> none
    pallas_call x1, Pallas kernels: 2.81 us -> 1.45 us  [local(): pl.pallas_call(own_kernel, out_shape=sums, in_specs=[vmem], out_specs=vmem)]
    reshape x2 -> x0, local copies, waits for them, and re-layouts: 1.34 us -> none  [the longest x1 0.67 us: local(): list_target.reshape(peers, slots)]
    concatenate x1 -> x0, other arithmetic: 0.74 us -> none  [local(): jnp.concatenate([jnp.concatenate([positions, masses[None, :]], 0), ids], 1)]
    pallas_call x0 -> x1, Pallas kernels: none -> 0.74 us  [local(): pl.pallas_call(pack_kernel, out_shape=pltpu.VMEM((4, bodies + block), f32...]
    convert_element_type x1 -> x0, other arithmetic: 0.68 us -> none  [local(): ids = jnp.pad(essential.astype(f32), ((0, 4 - levels), (0, block - picks)))]
  transfers between devices with their start and end apart: 6 -> 6, of which waited for: 3 -> 3; matrix products, arithmetic and copies ran while one was open for 6% -> 0% of each run, Pallas kernels for 26% -> 18%
where the time goes in v2:
time: 23.4 us; the launch traced here: 23.2 us
  Pallas kernels  8.97 us (38%)
  starting transfers between devices  8.87 us (38%)
  waiting for transfers between devices  4.65 us (20%)
  between operations  0.69 us (3%)
    ppermute x6, starting transfers between devices, exchange(): return lax.ppermute(value, axis, pairs)  8.87 us
    ppermute x6, waiting for transfers between devices, exchange(): return lax.ppermute(value, axis, pairs)  4.65 us
    pallas_call x1, Pallas kernels, local(): pl.pallas_call(remote_kernel, out_shape=(shape, shape), in_specs=[vmem, v...  4.1 us
    pallas_call x2, Pallas kernels, local(): pl.pallas_call(lambda own_ref, other_ref, sums_ref, out_ref, level=level:...  2.68 us
    pallas_call x1, Pallas kernels, local(): pl.pallas_call(own_kernel, out_shape=sums, in_specs=[vmem], out_specs=vmem)  1.45 us
    pallas_call x1, Pallas kernels, local(): pl.pallas_call(pack_kernel, out_shape=pltpu.VMEM((4, bodies + block), f32...  0.74 us
  transfers between devices with their start and end apart: 6, of which 3 were waited for; matrix products, arithmetic and copies ran while one was open for 0% of the time, Pallas kernels for 18%

profile of v2, /device:TPU:0, one launch (start us, length us, event | category | flops | bytes accessed | tf_op | source)
XLA Modules:
  0.0 23.2 jit_solution(2835507826195606706)
XLA Ops:
  0.6 0.7 %shard_map.86.own_ref = f32[4,1152]{1,0:T(4,128)S(1)} custom-call(s32[2,4]{1,0:T(2,128)} %essential_ref.1, f32[3,1024]{1,0:T(4,128)} %position_ref.1, f32[1,1024]{1,0:T(1,128)} %bitcast.16), custom_call_target="tpu_custom_call" | custom-call | tf_op jit(solution)/shard_map/pallas_call | solution.py:177
  1.4 3.0 %collective-permute-start = (f32[4,1152]{1,0:T(4,128)S(1)}, f32[4,1152]{1,0:T(4,128)S(1)}, u32[]{:S(2)}, u32[]{:S(2)}) collective-permute-start(f32[4,1152]{1,0:T(4,128)S(1)} %shard_map.86.own_ref), channel_id=1, source_target_pairs={{0,8},{4,12},{8,0},{12,4},{16,24},{20,28},{24,16},{28,20},{1,9},{5... | collective-permute-start | bytes 55304 | tf_op jit(solution)/shard_map/ppermute | solution.py:20
  4.4 1.5 %collective-permute-start.1 = (f32[4,1152]{1,0:T(4,128)S(1)}, f32[4,1152]{1,0:T(4,128)S(1)}, u32[]{:S(2)}, u32[]{:S(2)}) collective-permute-start(f32[4,1152]{1,0:T(4,128)S(1)} %shard_map.86.own_ref), channel_id=1, source_target_pairs={{0,16},{4,20},{8,24},{12,28},{16,0},{20,4},{24,8},{28,12},{1,17},{... | collective-permute-start | bytes 55304 | tf_op jit(solution)/shard_map/ppermute | solution.py:20
  5.9 0.0 collective-permute-start.2
  6.0 0.2 collective-permute-done
  6.2 2.0 %collective-permute-done.1 = f32[4,1152]{1,0:T(4,128)S(1)} collective-permute-done((f32[4,1152]{1,0:T(4,128)S(1)}, f32[4,1152]{1,0:T(4,128)S(1)}, u32[]{:S(2)}, u32[]{:S(2)}) %collective-permute-start.1) | collective-permute-done | bytes 18464 | tf_op jit(solution)/shard_map/ppermute | solution.py:20
  8.2 2.4 %collective-permute-done.2 = f32[4,1152]{1,0:T(4,128)S(1)} collective-permute-done((f32[4,1152]{1,0:T(4,128)S(1)}, f32[4,1152]{1,0:T(4,128)S(1)}, u32[]{:S(2)}, u32[]{:S(2)}) %collective-permute-start.2) | collective-permute-done | bytes 18464 | tf_op jit(solution)/shard_map/ppermute | solution.py:20
  10.6 0.1 collective-permute-start.3
  10.7 1.6 %collective-permute-start.5 = (f32[4,1152]{1,0:T(4,128)S(1)}, f32[4,1152]{1,0:T(4,128)S(1)}, u32[]{:S(2)}, u32[]{:S(2)}) collective-permute-start(f32[4,1152]{1,0:T(4,128)S(1)} %shard_map.86.own_ref), channel_id=1, source_target_pairs={{0,1},{1,0},{2,3},{3,2},{4,5},{5,4},{6,7},{7,6},{8,9},{9,8},{10,11... | collective-permute-start | bytes 55304 | tf_op jit(solution)/shard_map/ppermute | solution.py:20
  12.3 2.6 %collective-permute-start.4 = (f32[4,1152]{1,0:T(4,128)S(1)}, f32[4,1152]{1,0:T(4,128)S(1)}, u32[]{:S(2)}, u32[]{:S(2)}) collective-permute-start(f32[4,1152]{1,0:T(4,128)S(1)} %shard_map.86.own_ref), channel_id=1, source_target_pairs={{0,2},{1,3},{2,0},{3,1},{4,6},{5,7},{6,4},{7,5},{8,10},{9,11},{10,... | collective-permute-start | bytes 55304 | tf_op jit(solution)/shard_map/ppermute | solution.py:20
  14.9 1.4 %shard_map.87.sums_ref = f32[16,1024]{1,0:T(8,128)S(1)} custom-call(f32[4,1152]{1,0:T(4,128)S(1)} %shard_map.86.own_ref), custom_call_target="tpu_custom_call" | custom-call | tf_op jit(solution)/shard_map/pallas_call | solution.py:191
  16.4 0.0 collective-permute-done.5.other_ref
  16.4 1.3 %shard_map.88.sums_ref = f32[16,1024]{1,0:T(8,128)S(1)} custom-call(f32[4,1152]{1,0:T(4,128)S(1)} %shard_map.86.own_ref, f32[4,1152]{1,0:T(4,128)S(1)} %collective-permute-done.5.other_ref, f32[16,1024]{1,0:T(8,128)S(1)} %shard_map.87.sums_ref), custom_call_target="tpu_custom_call" | custom-call | tf_op jit(solution)/shard_map/pallas_call | solution.py:193
  17.7 0.0 collective-permute-done.4.other_ref
  17.7 1.3 %shard_map.89.sums_ref = f32[16,1024]{1,0:T(8,128)S(1)} custom-call(f32[4,1152]{1,0:T(4,128)S(1)} %shard_map.86.own_ref, f32[4,1152]{1,0:T(4,128)S(1)} %collective-permute-done.4.other_ref, f32[16,1024]{1,0:T(8,128)S(1)} %shard_map.88.sums_ref), custom_call_target="tpu_custom_call" | custom-call | tf_op jit(solution)/shard_map/pallas_call | solution.py:193
  19.1 0.0 collective-permute-done.3.there_ref
  19.1 4.1 %shard_map.90 = (f32[3,1024]{1,0:T(4,128)}, f32[3,1024]{1,0:T(4,128)}) custom-call(f32[4,4,1152]{2,1,0:T(4,128)S(1)} %pad_maximum_fusion.here_ref, f32[4,4,1152]{2,1,0:T(4,128)S(1)} %collective-permute-done.3.there_ref, s32[1,8]{1,0:T(1,128)} %bitcast.19, s32[4,8]{1,0:T(4,128)} %bitcast.17, s32[4,8]{1,0:T(4,128)} %bitcast.18, ...), custom_call_target="tpu_custom_call" | custom-call | tf_op jit(solution)/shard_map/pallas_call | solution.py:202
  (1 shorter events, 0.0 us)
Async XLA Ops:
  1.4 4.8 %collective-permute-start = (f32[4,1152]{1,0:T(4,128)S(1)}, f32[4,1152]{1,0:T(4,128)S(1)}, u32[]{:S(2)}, u32[]{:S(2)}) collective-permute-start(f32[4,1152]{1,0:T(4,128)S(1)} %shard_map.86.own_ref), channel_id=1, source_target_pairs={{0,8},{4,12},{8,0},{12,4},{16,24},{20,28},{24,16},{28,20},{1,9},{5... | collective-permute-start | bytes 55304 | tf_op jit(solution)/shard_map/ppermute | solution.py:20
  4.4 3.8 %collective-permute-start.1 = (f32[4,1152]{1,0:T(4,128)S(1)}, f32[4,1152]{1,0:T(4,128)S(1)}, u32[]{:S(2)}, u32[]{:S(2)}) collective-permute-start(f32[4,1152]{1,0:T(4,128)S(1)} %shard_map.86.own_ref), channel_id=1, source_target_pairs={{0,16},{4,20},{8,24},{12,28},{16,0},{20,4},{24,8},{28,12},{1,17},{... | collective-permute-start | bytes 55304 | tf_op jit(solution)/shard_map/ppermute | solution.py:20
  5.9 4.7 %collective-permute-start.2 = (f32[4,1152]{1,0:T(4,128)S(1)}, f32[4,1152]{1,0:T(4,128)S(1)}, u32[]{:S(2)}, u32[]{:S(2)}) collective-permute-start(f32[4,1152]{1,0:T(4,128)S(1)} %shard_map.86.own_ref), channel_id=1, source_target_pairs={{0,24},{4,28},{8,16},{12,20},{16,8},{20,12},{24,0},{28,4},{1,25},{... | collective-permute-start | bytes 55304 | tf_op jit(solution)/shard_map/ppermute | solution.py:20
  10.6 8.5 %collective-permute-start.3 = (f32[4,4,1152]{2,1,0:T(4,128)S(1)}, f32[4,4,1152]{2,1,0:T(4,128)S(1)}, u32[]{:S(2)}, u32[]{:S(2)}) collective-permute-start(f32[4,4,1152]{2,1,0:T(4,128)S(1)} %pad_maximum_fusion.here_ref), channel_id=1, source_target_pairs={{0,4},{4,0},{8,12},{12,8},{16,20},{20,16},{24,28},{28,24},{1,5},{5... | collective-permute-start | bytes 221192 | tf_op jit(solution)/shard_map/ppermute | solution.py:20
  10.7 5.7 %collective-permute-start.5 = (f32[4,1152]{1,0:T(4,128)S(1)}, f32[4,1152]{1,0:T(4,128)S(1)}, u32[]{:S(2)}, u32[]{:S(2)}) collective-permute-start(f32[4,1152]{1,0:T(4,128)S(1)} %shard_map.86.own_ref), channel_id=1, source_target_pairs={{0,1},{1,0},{2,3},{3,2},{4,5},{5,4},{6,7},{7,6},{8,9},{9,8},{10,11... | collective-permute-start | bytes 55304 | tf_op jit(solution)/shard_map/ppermute | solution.py:20
  12.3 5.4 %collective-permute-start.4 = (f32[4,1152]{1,0:T(4,128)S(1)}, f32[4,1152]{1,0:T(4,128)S(1)}, u32[]{:S(2)}, u32[]{:S(2)}) collective-permute-start(f32[4,1152]{1,0:T(4,128)S(1)} %shard_map.86.own_ref), channel_id=1, source_target_pairs={{0,2},{1,3},{2,0},{3,1},{4,6},{5,7},{6,4},{7,5},{8,10},{9,11},{10,... | collective-permute-start | bytes 55304 | tf_op jit(solution)/shard_map/ppermute | solution.py:20

commit v3 on v2

--- a/solution.py
+++ b/solution.py
@@ -1,3 +1,5 @@
+import functools
+
 import jax
 import jax.numpy as jnp
 from jax import lax
@@ -9,10 +11,13 @@
 soften_sq = 0.01
 time_step = 0.5
 block = 128
+cells = 32.0
+mark = 2.0**-7
 f32 = jnp.float32
 bf16 = jnp.bfloat16
 vmem = pl.BlockSpec(memory_space=pltpu.VMEM)
 smem = pl.BlockSpec(memory_space=pltpu.SMEM)
+hbm = pl.BlockSpec(memory_space=pl.ANY)
 
 
 def exchange(value, axis, mask):
@@ -20,29 +25,50 @@
     return lax.ppermute(value, axis, pairs)
 
 
+def rounded(value):
+    return value.astype(bf16).astype(f32)
+
+
 def split(value):
-    high = value.astype(bf16).astype(f32)
+    high = rounded(value)
     rest = value - high
-    mid = rest.astype(bf16).astype(f32)
+    mid = rounded(rest)
     return high, mid, rest - mid
 
 
+def on_grid(points):
+    row = lax.broadcasted_iota(jnp.int32, points.shape, 0)
+    points = jnp.where(row == 3, 1.0 + mark, points)
+    grid = jnp.round(points * cells) * (1.0 / cells)
+    rest = points - grid
+    high = rounded(rest)
+    norm = jnp.sum((grid * grid)[0:3], axis=0, keepdims=True)
+    coarse = rounded(norm)
+    fine = (norm - coarse) + jnp.sum(((2.0 * grid + rest) * rest)[0:3], axis=0, keepdims=True)
+    return grid, high, rest - high, coarse, fine
+
+
 def target_rows(points):
-    high, mid, low = split(-2.0 * points[0:3])
-    norm = jnp.sum(points[0:3] * points[0:3], axis=0, keepdims=True) + soften_sq
-    one = jnp.ones_like(norm)
-    return jnp.concatenate([high, mid, low, high, mid, high, one, one, one, *split(norm)], 0).astype(bf16)
+    grid, high, low, coarse, fine = on_grid(points)
+    grid, high, low = -2.0 * grid[0:3], -2.0 * high[0:3], -2.0 * low[0:3]
+    first, second, third = split(fine + soften_sq)
+    one, zero = jnp.ones_like(fine), jnp.zeros_like(fine)
+    return jnp.concatenate(
+        [grid, coarse, one, one, one, one, high, first, low, second]
+        + [grid, third * (1.0 / mark), grid, zero, high, zero, low, zero],
+        0,
+    ).astype(bf16)
 
 
 def source_rows(points):
-    high, mid, low = split(points[0:3])
-    norm = jnp.sum(points[0:3] * points[0:3], axis=0, keepdims=True)
-    one = jnp.ones_like(norm)
-    return jnp.concatenate([high, high, high, mid, mid, low, *split(norm), one, one, one], 0).astype(bf16)
+    grid, high, low, coarse, fine = on_grid(points)
+    scalars = jnp.concatenate([coarse, *split(fine)], 0)
+    return jnp.concatenate([grid, scalars, grid, grid, high, low, high, high], 0).astype(bf16)
 
 
 def moment_rows(points):
-    moments = jnp.concatenate([points[0:3] * points[3:4], points[3:4]], 0)
+    row = lax.broadcasted_iota(jnp.int32, points.shape, 0)
+    moments = jnp.where(row == 3, 1.0, points) * points[3:4]
     return jnp.concatenate([*split(moments), jnp.zeros_like(moments)], 0).astype(bf16)
 
 
@@ -96,13 +122,15 @@
     own_ref[:, bodies:] = codes
 
 
-def own_kernel(own_ref, out_ref):
+def own_kernel(own_ref, rows_ref, out_ref):
     own = own_ref[:, : out_ref.shape[1]]
-    out_ref[...] = pull_all(flip(source_rows(own)), moment_rows(own), target_rows(own))
-
-
-def partner_kernel(picks, own_ref, other_ref, level, sums_ref, out_ref):
-    bodies = out_ref.shape[1]
+    rows = target_rows(own)
+    rows_ref[...] = rows
+    out_ref[...] = pull_all(flip(source_rows(own)), moment_rows(own), rows)
+
+
+def partner_pulls(picks, level, other_ref, rows_ref):
+    bodies = rows_ref.shape[1]
     count = bodies // block
     other = other_ref[:, :bodies]
     lane = lax.broadcasted_iota(jnp.int32, (1, block), 1)
@@ -122,23 +150,36 @@
     near = [other_ref[:, pl.ds(pl.multiple_of(pick * block, block), block)] for pick in chosen]
     points = jnp.concatenate(near + [mono], 1)
     whole = picks * block
+    last = whole + (count + 15) // 16 * 16
     columns = flip(source_rows(points))
     moments = moment_rows(points)
-    targets = target_rows(own_ref[:, :bodies])
-    near = pull_all(columns[:whole], moments[:, :whole], targets)
-    far = pull(columns[whole : whole + 16], moments[:, whole : whole + 16], targets)
-    out_ref[...] = sums_ref[...] + near + far
-
-
-def remote_kernel(here_ref, there_ref, count_ref, target_ref, source_ref, sums_ref, speed_ref,
-                  position_ref, velocity_ref, rows_ref, acc_ref):
+    rows = rows_ref[...]
+    near = pull_all(columns[:whole], moments[:, :whole], rows)
+    return near + pull(columns[whole:last], moments[:, whole:last], rows)
+
+
+def partner_kernel(picks, level, rows_ref, other_ref, sums_ref, out_ref):
+    out_ref[...] = sums_ref[...] + partner_pulls(picks, level, other_ref, rows_ref)
+
+
+def remote_kernel(picks, level, rows_ref, other_ref, here_ref, there_ref, sums_ref, speed_ref,
+                  counts_ref, targets_ref, sources_ref, position_ref, velocity_ref,
+                  acc_ref, count_ref, target_ref, source_ref, done_ref):
+    lists = [
+        pltpu.make_async_copy(far, near, done_ref.at[index])
+        for index, (far, near) in enumerate(
+            [(counts_ref, count_ref), (targets_ref, target_ref), (sources_ref, source_ref)]
+        )
+    ]
+    for copy in lists:
+        copy.start()
     bodies = sums_ref.shape[1]
     slots = target_ref.shape[0]
     place = lax.axis_index("outer")
-    own = here_ref[0, :, :bodies]
-    rows_ref[...] = target_rows(own)
-    acc_ref[...] = sums_ref[...]
     half = here_ref.shape[0]
+    acc_ref[...] = sums_ref[...] + partner_pulls(picks, level, other_ref, rows_ref)
+    for copy in lists:
+        copy.wait()
 
     def peer(group_ref, index, mask):
         other = place ^ mask
@@ -161,7 +202,7 @@
     for index in range(half):
         peer(there_ref, index, 2 * index + 1)
     total = acc_ref[0:4] + acc_ref[4:8] + acc_ref[8:12]
-    position = own[0:3]
+    position = here_ref[0, 0:3, :bodies]
     velocity = speed_ref[...] + time_step * (total[0:3] - position * total[3:4])
     velocity_ref[...] = velocity
     position_ref[...] = position + time_step * velocity
@@ -188,31 +229,42 @@
         here.append(exchange(own, "outer", mask))
     here = jnp.stack(here)
     there = exchange(here, "outer", 1)
-    acc = pl.pallas_call(own_kernel, out_shape=sums, in_specs=[vmem], out_specs=vmem)(kept(own))
-    for level in range(levels):
+    rows, acc = pl.pallas_call(
+        own_kernel,
+        out_shape=(pltpu.VMEM((32, bodies), bf16), sums),
+        in_specs=[vmem],
+        out_specs=(vmem, vmem),
+    )(kept(own))
+    for level in range(levels - 1):
         acc = pl.pallas_call(
-            lambda own_ref, other_ref, sums_ref, out_ref, level=level: partner_kernel(
-                picks, own_ref, other_ref, level, sums_ref, out_ref
-            ),
+            functools.partial(partner_kernel, picks, level),
             out_shape=sums,
             in_specs=[vmem] * 3,
             out_specs=vmem,
-        )(kept(own), kept(across[level]), kept(acc))
+        )(kept(rows), kept(across[level]), kept(acc))
     shape = jax.ShapeDtypeStruct((3, bodies), f32)
     return pl.pallas_call(
-        remote_kernel,
+        functools.partial(remote_kernel, picks, levels - 1),
         out_shape=(shape, shape),
-        in_specs=[vmem, vmem, smem, smem, smem, vmem, vmem],
+        in_specs=[vmem] * 6 + [hbm] * 3,
         out_specs=(vmem, vmem),
-        scratch_shapes=[pltpu.VMEM((24, bodies), bf16), pltpu.VMEM((16, bodies), f32)],
+        scratch_shapes=[
+            pltpu.VMEM((16, bodies), f32),
+            pltpu.SMEM((1, peers), jnp.int32),
+            pltpu.SMEM((slots, peers), jnp.int32),
+            pltpu.SMEM((slots, peers), jnp.int32),
+            pltpu.SemaphoreType.DMA((3,)),
+        ],
     )(
+        kept(rows),
+        kept(across[levels - 1]),
         kept(here),
         kept(there),
+        kept(acc),
+        kept(velocities),
         list_count.T,
         list_target.reshape(peers, slots).T,
         list_source.reshape(peers, slots).T,
-        kept(acc),
-        velocities,
     )
 
 

time: 23.4 us -> 21.6 us (0.923)
  waiting for transfers between devices: 4.65 us -> 3.63 us
  Pallas kernels: 8.97 us -> 8.1 us
    ppermute x6, waiting for transfers between devices: 4.65 us -> 3.63 us  [exchange(): return lax.ppermute(value, axis, pairs)]
    pallas_call x4 -> x3, Pallas kernels: 8.23 us -> 7.36 us  [the longest x1 4.54 us: local(): pl.pallas_call(functools.partial(remote_kernel, picks, levels - 1), out_s...]
  transfers between devices with their start and end apart: 6 -> 6, of which waited for: 3 -> 3; matrix products, arithmetic and copies ran while one was open for 0% -> 0% of each run, Pallas kernels for 18% -> 13%
where the time goes in v3:
time: 21.6 us; the launch traced here: 21.4 us
  starting transfers between devices  8.93 us (41%)
  Pallas kernels  8.1 us (38%)
  waiting for transfers between devices  3.63 us (17%)
  between operations  0.69 us (3%)
    ppermute x6, starting transfers between devices, exchange(): return lax.ppermute(value, axis, pairs)  8.93 us
    pallas_call x1, Pallas kernels, local(): pl.pallas_call(functools.partial(remote_kernel, picks, levels - 1), out_s...  4.54 us
    ppermute x6, waiting for transfers between devices, exchange(): return lax.ppermute(value, axis, pairs)  3.63 us
    pallas_call x1, Pallas kernels, local(): pl.pallas_call(own_kernel, out_shape=(pltpu.VMEM((32, bodies), bf16), sum...  1.46 us
    pallas_call x1, Pallas kernels, local(): pl.pallas_call(functools.partial(partner_kernel, picks, level), out_shape...  1.36 us
    pallas_call x1, Pallas kernels, local(): pl.pallas_call(pack_kernel, out_shape=pltpu.VMEM((4, bodies + block), f32...  0.74 us
  transfers between devices with their start and end apart: 6, of which 3 were waited for; matrix products, arithmetic and copies ran while one was open for 0% of the time, Pallas kernels for 13%

profile of v3, /device:TPU:0, one launch (start us, length us, event | category | flops | bytes accessed | tf_op | source)
XLA Modules:
  0.0 21.4 jit_solution(12551156859520895458)
XLA Ops:
  0.6 0.7 %shard_map.86.own_ref = f32[4,1152]{1,0:T(4,128)S(1)} custom-call(s32[2,4]{1,0:T(2,128)} %essential_ref.1, f32[3,1024]{1,0:T(4,128)} %position_ref.1, f32[1,1024]{1,0:T(1,128)} %bitcast.16), custom_call_target="tpu_custom_call" | custom-call | tf_op jit(solution)/shard_map/pallas_call | solution.py:218
  1.4 4.0 %collective-permute-start.3 = (f32[4,1152]{1,0:T(4,128)S(1)}, f32[4,1152]{1,0:T(4,128)S(1)}, u32[]{:S(2)}, u32[]{:S(2)}) collective-permute-start(f32[4,1152]{1,0:T(4,128)S(1)} %shard_map.86.own_ref), channel_id=1, source_target_pairs={{0,24},{4,28},{8,16},{12,20},{16,8},{20,12},{24,0},{28,4},{1,25},{... | collective-permute-start | bytes 55304 | tf_op jit(solution)/shard_map/ppermute | solution.py:25
  5.4 0.5 %collective-permute-start.2 = (f32[4,1152]{1,0:T(4,128)S(1)}, f32[4,1152]{1,0:T(4,128)S(1)}, u32[]{:S(2)}, u32[]{:S(2)}) collective-permute-start(f32[4,1152]{1,0:T(4,128)S(1)} %shard_map.86.own_ref), channel_id=1, source_target_pairs={{0,16},{4,20},{8,24},{12,28},{16,0},{20,4},{24,8},{28,12},{1,17},{... | collective-permute-start | bytes 55304 | tf_op jit(solution)/shard_map/ppermute | solution.py:25
  5.9 0.1 collective-permute-start.1
  6.0 1.1 %collective-permute-done.3 = f32[4,1152]{1,0:T(4,128)S(1)} collective-permute-done((f32[4,1152]{1,0:T(4,128)S(1)}, f32[4,1152]{1,0:T(4,128)S(1)}, u32[]{:S(2)}, u32[]{:S(2)}) %collective-permute-start.3) | collective-permute-done | bytes 18464 | tf_op jit(solution)/shard_map/ppermute | solution.py:25
  7.1 2.0 %collective-permute-done.2 = f32[4,1152]{1,0:T(4,128)S(1)} collective-permute-done((f32[4,1152]{1,0:T(4,128)S(1)}, f32[4,1152]{1,0:T(4,128)S(1)}, u32[]{:S(2)}, u32[]{:S(2)}) %collective-permute-start.2) | collective-permute-done | bytes 18464 | tf_op jit(solution)/shard_map/ppermute | solution.py:25
  9.1 0.5 %collective-permute-done.1 = f32[4,1152]{1,0:T(4,128)S(1)} collective-permute-done((f32[4,1152]{1,0:T(4,128)S(1)}, f32[4,1152]{1,0:T(4,128)S(1)}, u32[]{:S(2)}, u32[]{:S(2)}) %collective-permute-start.1) | collective-permute-done | bytes 18464 | tf_op jit(solution)/shard_map/ppermute | solution.py:25
  9.7 0.1 collective-permute-start.4
  9.7 1.6 %collective-permute-start.5 = (f32[4,1152]{1,0:T(4,128)S(1)}, f32[4,1152]{1,0:T(4,128)S(1)}, u32[]{:S(2)}, u32[]{:S(2)}) collective-permute-start(f32[4,1152]{1,0:T(4,128)S(1)} %shard_map.86.own_ref), channel_id=1, source_target_pairs={{0,1},{1,0},{2,3},{3,2},{4,5},{5,4},{6,7},{7,6},{8,9},{9,8},{10,11... | collective-permute-start | bytes 55304 | tf_op jit(solution)/shard_map/ppermute | solution.py:25
  11.4 2.6 %collective-permute-start = (f32[4,1152]{1,0:T(4,128)S(1)}, f32[4,1152]{1,0:T(4,128)S(1)}, u32[]{:S(2)}, u32[]{:S(2)}) collective-permute-start(f32[4,1152]{1,0:T(4,128)S(1)} %shard_map.86.own_ref), channel_id=1, source_target_pairs={{0,2},{1,3},{2,0},{3,1},{4,6},{5,7},{6,4},{7,5},{8,10},{9,11},{10,... | collective-permute-start | bytes 55304 | tf_op jit(solution)/shard_map/ppermute | solution.py:25
  14.0 1.5 %shard_map.87 = (bf16[32,1024]{1,0:T(8,128)(2,1)S(1)}, f32[16,1024]{1,0:T(8,128)S(1)}) custom-call(f32[4,1152]{1,0:T(4,128)S(1)} %shard_map.86.own_ref), custom_call_target="tpu_custom_call" | custom-call | tf_op jit(solution)/shard_map/pallas_call | solution.py:232
  15.4 0.0 collective-permute-done.5.other_ref
  15.4 0.0 copy-start
  15.4 1.4 %shard_map.88.sums_ref = f32[16,1024]{1,0:T(8,128)S(1)} custom-call(bf16[32,1024]{1,0:T(8,128)(2,1)S(1)} %get-tuple-element.4.rows_ref, f32[4,1152]{1,0:T(4,128)S(1)} %collective-permute-done.5.other_ref, f32[16,1024]{1,0:T(8,128)S(1)} %get-tuple-element.5.sums_ref), custom_call_target="tpu_custom_call" | custom-call | tf_op jit(solution)/shard_map/pallas_call | solution.py:239
  16.8 0.0 collective-permute-done.other_ref
  16.8 0.0 collective-permute-done.4.there_ref
  16.8 0.0 copy-done
  16.8 4.5 %shard_map.89 = (f32[3,1024]{1,0:T(4,128)}, f32[3,1024]{1,0:T(4,128)}) custom-call(bf16[32,1024]{1,0:T(8,128)(2,1)S(1)} %get-tuple-element.4.rows_ref, f32[4,1152]{1,0:T(4,128)S(1)} %collective-permute-done.other_ref, f32[4,4,1152]{2,1,0:T(4,128)S(1)} %pad_maximum_fusion.here_ref, f32[4,4,1152]{2,1,0:T(4,128)S(1)} %collective-permute-done.4.there_ref, ...), custom_call_target="tpu_custom_call" | custom-call | tf_op jit(solution)/shard_map/pallas_call | solution.py:246
  (1 shorter events, 0.0 us)
Async XLA Ops:
  1.4 5.7 %collective-permute-start.3 = (f32[4,1152]{1,0:T(4,128)S(1)}, f32[4,1152]{1,0:T(4,128)S(1)}, u32[]{:S(2)}, u32[]{:S(2)}) collective-permute-start(f32[4,1152]{1,0:T(4,128)S(1)} %shard_map.86.own_ref), channel_id=1, source_target_pairs={{0,24},{4,28},{8,16},{12,20},{16,8},{20,12},{24,0},{28,4},{1,25},{... | collective-permute-start | bytes 55304 | tf_op jit(solution)/shard_map/ppermute | solution.py:25
  5.4 3.8 %collective-permute-start.2 = (f32[4,1152]{1,0:T(4,128)S(1)}, f32[4,1152]{1,0:T(4,128)S(1)}, u32[]{:S(2)}, u32[]{:S(2)}) collective-permute-start(f32[4,1152]{1,0:T(4,128)S(1)} %shard_map.86.own_ref), channel_id=1, source_target_pairs={{0,16},{4,20},{8,24},{12,28},{16,0},{20,4},{24,8},{28,12},{1,17},{... | collective-permute-start | bytes 55304 | tf_op jit(solution)/shard_map/ppermute | solution.py:25
  5.9 3.8 %collective-permute-start.1 = (f32[4,1152]{1,0:T(4,128)S(1)}, f32[4,1152]{1,0:T(4,128)S(1)}, u32[]{:S(2)}, u32[]{:S(2)}) collective-permute-start(f32[4,1152]{1,0:T(4,128)S(1)} %shard_map.86.own_ref), channel_id=1, source_target_pairs={{0,8},{4,12},{8,0},{12,4},{16,24},{20,28},{24,16},{28,20},{1,9},{5... | collective-permute-start | bytes 55304 | tf_op jit(solution)/shard_map/ppermute | solution.py:25
  9.7 7.2 %collective-permute-start.4 = (f32[4,4,1152]{2,1,0:T(4,128)S(1)}, f32[4,4,1152]{2,1,0:T(4,128)S(1)}, u32[]{:S(2)}, u32[]{:S(2)}) collective-permute-start(f32[4,4,1152]{2,1,0:T(4,128)S(1)} %pad_maximum_fusion.here_ref), channel_id=1, source_target_pairs={{0,4},{4,0},{8,12},{12,8},{16,20},{20,16},{24,28},{28,24},{1,5},{5... | collective-permute-start | bytes 221192 | tf_op jit(solution)/shard_map/ppermute | solution.py:25
  9.7 5.7 %collective-permute-start.5 = (f32[4,1152]{1,0:T(4,128)S(1)}, f32[4,1152]{1,0:T(4,128)S(1)}, u32[]{:S(2)}, u32[]{:S(2)}) collective-permute-start(f32[4,1152]{1,0:T(4,128)S(1)} %shard_map.86.own_ref), channel_id=1, source_target_pairs={{0,1},{1,0},{2,3},{3,2},{4,5},{5,4},{6,7},{7,6},{8,9},{9,8},{10,11... | collective-permute-start | bytes 55304 | tf_op jit(solution)/shard_map/ppermute | solution.py:25
  11.4 5.4 %collective-permute-start = (f32[4,1152]{1,0:T(4,128)S(1)}, f32[4,1152]{1,0:T(4,128)S(1)}, u32[]{:S(2)}, u32[]{:S(2)}) collective-permute-start(f32[4,1152]{1,0:T(4,128)S(1)} %shard_map.86.own_ref), channel_id=1, source_target_pairs={{0,2},{1,3},{2,0},{3,1},{4,6},{5,7},{6,4},{7,5},{8,10},{9,11},{10,... | collective-permute-start | bytes 55304 | tf_op jit(solution)/shard_map/ppermute | solution.py:25
  15.4 1.4 %copy-start = (f32[3,1024]{1,0:T(4,128)S(1)}, f32[3,1024]{1,0:T(4,128)}, u32[]{:S(2)}) copy-start(f32[3,1024]{1,0:T(4,128)} %speed_ref.1) | copy-start | bytes 36868

commit v4 on v3

--- a/solution.py
+++ b/solution.py
@@ -72,8 +72,11 @@
     return jnp.concatenate([*split(moments), jnp.zeros_like(moments)], 0).astype(bf16)
 
 
-def pull(columns, moments, targets):
-    dist = jnp.dot(columns, targets, preferred_element_type=f32)
+def distances(columns, targets):
+    return jnp.dot(columns, targets, preferred_element_type=f32)
+
+
+def weighted(moments, dist):
     inverse = lax.rsqrt(dist)
     weight = inverse * inverse * inverse
     high = weight.astype(bf16)
@@ -83,23 +86,47 @@
     )
 
 
+def staged(tasks, depth):
+    waiting = []
+    for start, finish in tasks:
+        waiting.append((start(), finish))
+        if len(waiting) > depth:
+            dist, done = waiting.pop(0)
+            done(dist)
+    for dist, done in waiting:
+        done(dist)
+
+
 def flip(rows):
     return jnp.transpose(rows.astype(f32)).astype(bf16)
 
 
-def pull_all(columns, moments, targets, step=256):
-    parts = []
-    for start in range(0, targets.shape[1], step):
-        acc = None
-        for first in range(0, columns.shape[0], step):
-            part = pull(
-                columns[first : first + step],
-                moments[:, first : first + step],
-                targets[:, start : start + step],
-            )
-            acc = part if acc is None else acc + part
-        parts.append(acc)
-    return jnp.concatenate(parts, 1)
+def pull_tasks(columns, moments, targets, store, tile=256, step=256):
+    def task(start, first, last):
+        def begin():
+            return distances(columns[first:last], targets[:, start : start + tile])
+
+        def end(dist):
+            store(start, weighted(moments[:, first:last], dist))
+
+        return begin, end
+
+    total = columns.shape[0]
+    return [
+        task(start, first, min(first + step, total))
+        for start in range(0, targets.shape[1], tile)
+        for first in range(0, total, step)
+    ]
+
+
+def pull_all(columns, moments, targets, depth):
+    parts = {}
+
+    def store(start, part):
+        parts[start] = parts[start] + part if start in parts else part
+
+    staged(pull_tasks(columns, moments, targets, store), depth)
+    return jnp.concatenate([parts[start] for start in sorted(parts)], 1)
 
 
 def kept(value):
@@ -126,7 +153,7 @@
     own = own_ref[:, : out_ref.shape[1]]
     rows = target_rows(own)
     rows_ref[...] = rows
-    out_ref[...] = pull_all(flip(source_rows(own)), moment_rows(own), rows)
+    out_ref[...] = pull_all(flip(source_rows(own)), moment_rows(own), rows, 1)
 
 
 def partner_pulls(picks, level, other_ref, rows_ref):
@@ -154,8 +181,9 @@
     columns = flip(source_rows(points))
     moments = moment_rows(points)
     rows = rows_ref[...]
-    near = pull_all(columns[:whole], moments[:, :whole], rows)
-    return near + pull(columns[whole:last], moments[:, whole:last], rows)
+    near = pull_all(columns[:whole], moments[:, :whole], rows, 2)
+    far = weighted(moments[:, whole:last], distances(columns[whole:last], rows))
+    return near + far
 
 
 def partner_kernel(picks, level, rows_ref, other_ref, sums_ref, out_ref):
@@ -190,17 +218,25 @@
         points = jnp.concatenate(points, 1)
         columns = flip(source_rows(points))
         moments = moment_rows(points)
-        for slot in range(slots):
+
+        def task(slot):
             start = pl.multiple_of(target_ref[slot, other] * block, block)
             span = slice(slot * block, (slot + 1) * block)
-            part = pull(columns[span], moments[:, span], rows_ref[:, pl.ds(start, block)])
-            valid = jnp.where(slot < count_ref[0, other], 1.0, 0.0)
-            acc_ref[:, pl.ds(start, block)] += part * valid
-
-    for index in range(1, half):
-        peer(here_ref, index, 2 * index)
-    for index in range(half):
-        peer(there_ref, index, 2 * index + 1)
+
+            def begin():
+                return distances(columns[span], rows_ref[:, pl.ds(start, block)])
+
+            def end(dist):
+                valid = jnp.where(slot < count_ref[0, other], 1.0, 0.0)
+                acc_ref[:, pl.ds(start, block)] += weighted(moments[:, span], dist) * valid
+
+            return begin, end
+
+        return [task(slot) for slot in range(slots)]
+
+    peers = [(here_ref, index, 2 * index) for index in range(1, half)]
+    peers += [(there_ref, index, 2 * index + 1) for index in range(half)]
+    staged((task for item in peers for task in peer(*item)), 8)
     total = acc_ref[0:4] + acc_ref[4:8] + acc_ref[8:12]
     position = here_ref[0, 0:3, :bodies]
     velocity = speed_ref[...] + time_step * (total[0:3] - position * total[3:4])

time: 21.6 us -> 19.6 us (0.907)
  Pallas kernels: 8.1 us -> 6.18 us
    pallas_call x1, Pallas kernels: 4.54 us -> 2.84 us  [local(): pl.pallas_call(functools.partial(remote_kernel, picks, levels - 1), out_s...]
    pallas_call x1, Pallas kernels: 1.36 us -> 1.13 us  [local(): pl.pallas_call(functools.partial(partner_kernel, picks, level), out_shape...]
where the time goes in v4:
time: 19.6 us; the launch traced here: 19.5 us
  starting transfers between devices  8.93 us (46%)
  Pallas kernels  6.18 us (32%)
  waiting for transfers between devices  3.63 us (19%)
  between operations  0.69 us (4%)
    ppermute x6, starting transfers between devices, exchange(): return lax.ppermute(value, axis, pairs)  8.93 us
    ppermute x6, waiting for transfers between devices, exchange(): return lax.ppermute(value, axis, pairs)  3.63 us
    pallas_call x1, Pallas kernels, local(): pl.pallas_call(functools.partial(remote_kernel, picks, levels - 1), out_s...  2.84 us
    pallas_call x1, Pallas kernels, local(): pl.pallas_call(own_kernel, out_shape=(pltpu.VMEM((32, bodies), bf16), sum...  1.46 us
    pallas_call x1, Pallas kernels, local(): pl.pallas_call(functools.partial(partner_kernel, picks, level), out_shape...  1.13 us
    pallas_call x1, Pallas kernels, local(): pl.pallas_call(pack_kernel, out_shape=pltpu.VMEM((4, bodies + block), f32...  0.74 us
  transfers between devices with their start and end apart: 6, of which 3 were waited for; matrix products, arithmetic and copies ran while one was open for 0% of the time, Pallas kernels for 13%

profile of v4, /device:TPU:0, one launch (start us, length us, event | category | flops | bytes accessed | tf_op | source)
XLA Modules:
  0.0 19.5 jit_solution(13574586127240135176)
XLA Ops:
  0.6 0.7 %shard_map.86.own_ref = f32[4,1152]{1,0:T(4,128)S(1)} custom-call(s32[2,4]{1,0:T(2,128)} %essential_ref.1, f32[3,1024]{1,0:T(4,128)} %position_ref.1, f32[1,1024]{1,0:T(1,128)} %bitcast.16), custom_call_target="tpu_custom_call" | custom-call | tf_op jit(solution)/shard_map/pallas_call | solution.py:254
  1.4 4.0 %collective-permute-start.3 = (f32[4,1152]{1,0:T(4,128)S(1)}, f32[4,1152]{1,0:T(4,128)S(1)}, u32[]{:S(2)}, u32[]{:S(2)}) collective-permute-start(f32[4,1152]{1,0:T(4,128)S(1)} %shard_map.86.own_ref), channel_id=1, source_target_pairs={{0,24},{4,28},{8,16},{12,20},{16,8},{20,12},{24,0},{28,4},{1,25},{... | collective-permute-start | bytes 55304 | tf_op jit(solution)/shard_map/ppermute | solution.py:25
  5.4 0.5 %collective-permute-start.2 = (f32[4,1152]{1,0:T(4,128)S(1)}, f32[4,1152]{1,0:T(4,128)S(1)}, u32[]{:S(2)}, u32[]{:S(2)}) collective-permute-start(f32[4,1152]{1,0:T(4,128)S(1)} %shard_map.86.own_ref), channel_id=1, source_target_pairs={{0,16},{4,20},{8,24},{12,28},{16,0},{20,4},{24,8},{28,12},{1,17},{... | collective-permute-start | bytes 55304 | tf_op jit(solution)/shard_map/ppermute | solution.py:25
  5.9 0.1 collective-permute-start.1
  6.0 1.1 %collective-permute-done.3 = f32[4,1152]{1,0:T(4,128)S(1)} collective-permute-done((f32[4,1152]{1,0:T(4,128)S(1)}, f32[4,1152]{1,0:T(4,128)S(1)}, u32[]{:S(2)}, u32[]{:S(2)}) %collective-permute-start.3) | collective-permute-done | bytes 18464 | tf_op jit(solution)/shard_map/ppermute | solution.py:25
  7.1 2.0 %collective-permute-done.2 = f32[4,1152]{1,0:T(4,128)S(1)} collective-permute-done((f32[4,1152]{1,0:T(4,128)S(1)}, f32[4,1152]{1,0:T(4,128)S(1)}, u32[]{:S(2)}, u32[]{:S(2)}) %collective-permute-start.2) | collective-permute-done | bytes 18464 | tf_op jit(solution)/shard_map/ppermute | solution.py:25
  9.1 0.5 %collective-permute-done.1 = f32[4,1152]{1,0:T(4,128)S(1)} collective-permute-done((f32[4,1152]{1,0:T(4,128)S(1)}, f32[4,1152]{1,0:T(4,128)S(1)}, u32[]{:S(2)}, u32[]{:S(2)}) %collective-permute-start.1) | collective-permute-done | bytes 18464 | tf_op jit(solution)/shard_map/ppermute | solution.py:25
  9.7 0.1 collective-permute-start.4
  9.7 1.6 %collective-permute-start.5 = (f32[4,1152]{1,0:T(4,128)S(1)}, f32[4,1152]{1,0:T(4,128)S(1)}, u32[]{:S(2)}, u32[]{:S(2)}) collective-permute-start(f32[4,1152]{1,0:T(4,128)S(1)} %shard_map.86.own_ref), channel_id=1, source_target_pairs={{0,1},{1,0},{2,3},{3,2},{4,5},{5,4},{6,7},{7,6},{8,9},{9,8},{10,11... | collective-permute-start | bytes 55304 | tf_op jit(solution)/shard_map/ppermute | solution.py:25
  11.4 2.6 %collective-permute-start = (f32[4,1152]{1,0:T(4,128)S(1)}, f32[4,1152]{1,0:T(4,128)S(1)}, u32[]{:S(2)}, u32[]{:S(2)}) collective-permute-start(f32[4,1152]{1,0:T(4,128)S(1)} %shard_map.86.own_ref), channel_id=1, source_target_pairs={{0,2},{1,3},{2,0},{3,1},{4,6},{5,7},{6,4},{7,5},{8,10},{9,11},{10,... | collective-permute-start | bytes 55304 | tf_op jit(solution)/shard_map/ppermute | solution.py:25
  14.0 1.5 %shard_map.87 = (bf16[32,1024]{1,0:T(8,128)(2,1)S(1)}, f32[16,1024]{1,0:T(8,128)S(1)}) custom-call(f32[4,1152]{1,0:T(4,128)S(1)} %shard_map.86.own_ref), custom_call_target="tpu_custom_call" | custom-call | tf_op jit(solution)/shard_map/pallas_call | solution.py:268
  15.4 0.0 collective-permute-done.5.other_ref
  15.4 0.0 copy-start
  15.4 1.1 %shard_map.88.sums_ref = f32[16,1024]{1,0:T(8,128)S(1)} custom-call(bf16[32,1024]{1,0:T(8,128)(2,1)S(1)} %get-tuple-element.4.rows_ref, f32[4,1152]{1,0:T(4,128)S(1)} %collective-permute-done.5.other_ref, f32[16,1024]{1,0:T(8,128)S(1)} %get-tuple-element.5.sums_ref), custom_call_target="tpu_custom_call" | custom-call | tf_op jit(solution)/shard_map/pallas_call | solution.py:275
  16.6 0.0 collective-permute-done.other_ref
  16.6 0.0 collective-permute-done.4.there_ref
  16.6 0.0 copy-done
  16.6 2.8 %shard_map.89 = (f32[3,1024]{1,0:T(4,128)}, f32[3,1024]{1,0:T(4,128)}) custom-call(bf16[32,1024]{1,0:T(8,128)(2,1)S(1)} %get-tuple-element.4.rows_ref, f32[4,1152]{1,0:T(4,128)S(1)} %collective-permute-done.other_ref, f32[4,4,1152]{2,1,0:T(4,128)S(1)} %pad_maximum_fusion.here_ref, f32[4,4,1152]{2,1,0:T(4,128)S(1)} %collective-permute-done.4.there_ref, ...), custom_call_target="tpu_custom_call" | custom-call | tf_op jit(solution)/shard_map/pallas_call | solution.py:282
  (1 shorter events, 0.0 us)
Async XLA Ops:
  1.4 5.7 %collective-permute-start.3 = (f32[4,1152]{1,0:T(4,128)S(1)}, f32[4,1152]{1,0:T(4,128)S(1)}, u32[]{:S(2)}, u32[]{:S(2)}) collective-permute-start(f32[4,1152]{1,0:T(4,128)S(1)} %shard_map.86.own_ref), channel_id=1, source_target_pairs={{0,24},{4,28},{8,16},{12,20},{16,8},{20,12},{24,0},{28,4},{1,25},{... | collective-permute-start | bytes 55304 | tf_op jit(solution)/shard_map/ppermute | solution.py:25
  5.4 3.8 %collective-permute-start.2 = (f32[4,1152]{1,0:T(4,128)S(1)}, f32[4,1152]{1,0:T(4,128)S(1)}, u32[]{:S(2)}, u32[]{:S(2)}) collective-permute-start(f32[4,1152]{1,0:T(4,128)S(1)} %shard_map.86.own_ref), channel_id=1, source_target_pairs={{0,16},{4,20},{8,24},{12,28},{16,0},{20,4},{24,8},{28,12},{1,17},{... | collective-permute-start | bytes 55304 | tf_op jit(solution)/shard_map/ppermute | solution.py:25
  5.9 3.8 %collective-permute-start.1 = (f32[4,1152]{1,0:T(4,128)S(1)}, f32[4,1152]{1,0:T(4,128)S(1)}, u32[]{:S(2)}, u32[]{:S(2)}) collective-permute-start(f32[4,1152]{1,0:T(4,128)S(1)} %shard_map.86.own_ref), channel_id=1, source_target_pairs={{0,8},{4,12},{8,0},{12,4},{16,24},{20,28},{24,16},{28,20},{1,9},{5... | collective-permute-start | bytes 55304 | tf_op jit(solution)/shard_map/ppermute | solution.py:25
  9.7 6.9 %collective-permute-start.4 = (f32[4,4,1152]{2,1,0:T(4,128)S(1)}, f32[4,4,1152]{2,1,0:T(4,128)S(1)}, u32[]{:S(2)}, u32[]{:S(2)}) collective-permute-start(f32[4,4,1152]{2,1,0:T(4,128)S(1)} %pad_maximum_fusion.here_ref), channel_id=1, source_target_pairs={{0,4},{4,0},{8,12},{12,8},{16,20},{20,16},{24,28},{28,24},{1,5},{5... | collective-permute-start | bytes 221192 | tf_op jit(solution)/shard_map/ppermute | solution.py:25
  9.7 5.7 %collective-permute-start.5 = (f32[4,1152]{1,0:T(4,128)S(1)}, f32[4,1152]{1,0:T(4,128)S(1)}, u32[]{:S(2)}, u32[]{:S(2)}) collective-permute-start(f32[4,1152]{1,0:T(4,128)S(1)} %shard_map.86.own_ref), channel_id=1, source_target_pairs={{0,1},{1,0},{2,3},{3,2},{4,5},{5,4},{6,7},{7,6},{8,9},{9,8},{10,11... | collective-permute-start | bytes 55304 | tf_op jit(solution)/shard_map/ppermute | solution.py:25
  11.4 5.2 %collective-permute-start = (f32[4,1152]{1,0:T(4,128)S(1)}, f32[4,1152]{1,0:T(4,128)S(1)}, u32[]{:S(2)}, u32[]{:S(2)}) collective-permute-start(f32[4,1152]{1,0:T(4,128)S(1)} %shard_map.86.own_ref), channel_id=1, source_target_pairs={{0,2},{1,3},{2,0},{3,1},{4,6},{5,7},{6,4},{7,5},{8,10},{9,11},{10,... | collective-permute-start | bytes 55304 | tf_op jit(solution)/shard_map/ppermute | solution.py:25
  15.4 1.2 %copy-start = (f32[3,1024]{1,0:T(4,128)S(1)}, f32[3,1024]{1,0:T(4,128)}, u32[]{:S(2)}) copy-start(f32[3,1024]{1,0:T(4,128)} %speed_ref.1) | copy-start | bytes 36868
